TPU v7x, 32 devices: a whole 2x2x4 slice. The times are simulated.
32 devices in a mesh: wide: 8 (over z, y), narrow: 4 (over x, core).
Axes of the slice: x: 2, y: 2, z: 4, core: 2. Of those that a mesh axis runs over, the one named last changes fastest.
Arguments:
- tokens: bfloat16 [16384, 768], P(('wide', 'narrow')), may hold values from -6 to 6
- item_lengths: int32 [32], P('wide'), may hold values from 0 to 1024, as said below
- w_query: bfloat16 [768, 768], P(None, 'narrow'), may hold values from -0.3125 to 0.3125
- b_query: bfloat16 [768], P('narrow'), may hold values from -1.25 to 1.25
- w_key: bfloat16 [768, 768], P(None, 'narrow'), may hold values from -0.3125 to 0.3125
- w_value: bfloat16 [768, 768], P(None, 'narrow'), may hold values from -0.21875 to 0.21875
- b_value: bfloat16 [768], P('narrow'), may hold values from -1.25 to 1.25
- w_out: bfloat16 [768, 768], P('narrow'), may hold values from -0.875 to 0.875
- b_out: bfloat16 [768], replicated, may hold values from -1.25 to 1.25
- gain_attn: bfloat16 [768], replicated, may hold values from 0.5 to 1.5
- shift_attn: bfloat16 [768], replicated, may hold values from -1.25 to 1.25
- w_up: bfloat16 [768, 3072], P(None, 'narrow'), may hold values from -0.21875 to 0.21875
- b_up: bfloat16 [3072], P('narrow'), may hold values from -1.25 to 1.25
- w_down: bfloat16 [3072, 768], P('narrow'), may hold values from -0.109375 to 0.109375
- b_down: bfloat16 [768], replicated, may hold values from -1.25 to 1.25
- gain_ffn: bfloat16 [768], replicated, may hold values from 0.5 to 1.5
- shift_ffn: bfloat16 [768], replicated, may hold values from -1.25 to 1.25
- out_grad: bfloat16 [16384, 768], P(('wide', 'narrow')), may hold values from -6 to 6
Outputs:
- layer_out: bfloat16 [16384, 768], P(('wide', 'narrow'))
- token_grad: float32 [16384, 768], P(('wide', 'narrow'))
- w_query_grad: float32 [768, 768], P(None, 'narrow')
- b_query_grad: float32 [768], P('narrow')
- w_key_grad: float32 [768, 768], P(None, 'narrow')
- w_value_grad: float32 [768, 768], P(None, 'narrow')
- b_value_grad: float32 [768], P('narrow')
- w_out_grad: float32 [768, 768], P('narrow')
- b_out_grad: float32 [768], replicated
- gain_attn_grad: float32 [768], replicated
- shift_attn_grad: float32 [768], replicated
- w_up_grad: float32 [768, 3072], P(None, 'narrow')
- b_up_grad: float32 [3072], P('narrow')
- w_down_grad: float32 [3072, 768], P('narrow')
- b_down_grad: float32 [768], replicated
- gain_ffn_grad: float32 [768], replicated
- shift_ffn_grad: float32 [768], replicated
Inputs may be any that keep to these rules, and one draw needn't show every extreme that they name: `item_lengths`: the 4 entries of each index of wide list its items in token order, each of 512 or 1024 tokens, together 2048, followed by zeros; some index of wide holds only items of 1024 tokens.
All inputs are finite; a program needn't handle non-finite values.
Results may differ from a plain program's by a relative error of at most 0.02.
Values may be sent and summed in bfloat16 or wider, within the bound.
No kernel may reach another device: no remote copies, remote signals or barrier semaphores. Data moves between devices by JAX's collectives and lax.ppermute only.
A program may use at most 128 MiB of HBM per device.

v0:
```python
import jax
import jax.numpy as jnp
from jax import lax
from jax.sharding import PartitionSpec as P

HD = 64
BLOCK = 512


norm_eps = 1e-12
masked_score = -1e30
half_root = 0.7071067811865476
inv_root_two_pi = 0.3989422804014327


def item_layout(item_lengths, block_rows, block_count):
    item_ends = jnp.cumsum(item_lengths)
    item_starts = item_ends - item_lengths
    block_first = jnp.arange(block_count, dtype=jnp.int32) * block_rows
    owner_item = jnp.sum((item_ends[None, :] <= block_first[:, None]).astype(jnp.int32), axis=1)
    picker = owner_item[:, None] == jnp.arange(item_lengths.shape[0], dtype=jnp.int32)[None, :]
    block_start = jnp.sum(jnp.where(picker, item_starts[None, :], 0), axis=1)
    block_length = jnp.sum(jnp.where(picker, item_lengths[None, :], 0), axis=1)
    return (block_start, block_length)


def layer_norm(residual, gain_vec, shift_vec):
    centre = jnp.mean(residual, axis=1, keepdims=True)
    spread = residual - centre
    inverse = lax.rsqrt(jnp.mean(spread * spread, axis=1, keepdims=True) + norm_eps)
    unit_rows = spread * inverse
    return (
        unit_rows * gain_vec.astype(jnp.float32) + shift_vec.astype(jnp.float32),
        unit_rows,
        inverse,
    )


def norm_backward(upstream, unit_rows, inverse, gain_vec):
    gain_part = jnp.sum(upstream * unit_rows, axis=0)
    shift_part = jnp.sum(upstream, axis=0)
    unit_grad = upstream * gain_vec.astype(jnp.float32)
    residual_grad = inverse * (
        unit_grad
        - jnp.mean(unit_grad, axis=1, keepdims=True)
        - unit_rows * jnp.mean(unit_grad * unit_rows, axis=1, keepdims=True)
    )
    return (residual_grad, gain_part, shift_part)


def gelu_slope(values):
    return (
        0.5 * lax.erfc(-values * half_root)
        + values * jnp.exp(-0.5 * values * values) * inv_root_two_pi
    )


def block_scores(query_block, key_rows, item_start, item_length, window_start, window_rows):
    head_count = query_block.shape[1] // HD
    window_keys = lax.dynamic_slice_in_dim(key_rows, window_start, window_rows, 0).reshape(
        window_rows, head_count, HD
    )
    queries = query_block.reshape(query_block.shape[0], head_count, HD)
    raw_scores = jnp.einsum(
        "qhd,khd->hqk", queries, window_keys, preferred_element_type=jnp.float32
    ) * HD ** (-0.5)
    positions = window_start + jnp.arange(window_rows, dtype=jnp.int32)
    inside = (positions >= item_start) & (positions < item_start + item_length)
    return jnp.where(inside[None, None, :], raw_scores, masked_score)


def forward_block(
    query_block, key_rows, value_rows, item_start, item_length, window_start, window_rows
):
    block_len, head_cols = query_block.shape
    head_count = head_cols // HD
    scores = block_scores(query_block, key_rows, item_start, item_length, window_start, window_rows)
    row_top = jnp.max(scores, axis=2, keepdims=True)
    shifted = jnp.exp(scores - row_top)
    row_total = jnp.sum(shifted, axis=2, keepdims=True)
    probabilities = (shifted / row_total).astype(jnp.bfloat16)
    window_values = lax.dynamic_slice_in_dim(value_rows, window_start, window_rows, 0).reshape(
        window_rows, head_count, HD
    )
    context = jnp.einsum(
        "hqk,khd->qhd", probabilities, window_values, preferred_element_type=jnp.float32
    )
    return (
        context.reshape(block_len, head_cols).astype(jnp.bfloat16),
        (row_top + jnp.log(row_total))[:, :, 0],
    )


def backward_block(
    running,
    query_block,
    grad_block,
    row_lse,
    item_start,
    item_length,
    key_rows,
    value_rows,
    window_start,
    window_rows,
):
    key_acc, value_acc = running
    block_len, head_cols = query_block.shape
    head_count = head_cols // HD
    score_scale = HD ** (-0.5)
    scores = block_scores(query_block, key_rows, item_start, item_length, window_start, window_rows)
    probabilities = jnp.exp(scores - row_lse[:, :, None])
    window_keys = lax.dynamic_slice_in_dim(key_rows, window_start, window_rows, 0).reshape(
        window_rows, head_count, HD
    )
    window_values = lax.dynamic_slice_in_dim(value_rows, window_start, window_rows, 0).reshape(
        window_rows, head_count, HD
    )
    queries = query_block.reshape(block_len, head_count, HD)
    grads_in = grad_block.reshape(block_len, head_count, HD)
    prob_grad = jnp.einsum(
        "qhd,khd->hqk", grads_in, window_values, preferred_element_type=jnp.float32
    )
    row_dot = jnp.sum(probabilities * prob_grad, axis=2, keepdims=True)
    score_grad = (probabilities * (prob_grad - row_dot)).astype(jnp.bfloat16)
    query_grad = (
        jnp.einsum("hqk,khd->qhd", score_grad, window_keys, preferred_element_type=jnp.float32)
        * score_scale
    )
    key_part = (
        jnp.einsum("hqk,qhd->khd", score_grad, queries, preferred_element_type=jnp.float32)
        * score_scale
    )
    value_part = jnp.einsum(
        "hqk,qhd->khd",
        probabilities.astype(jnp.bfloat16),
        grads_in,
        preferred_element_type=jnp.float32,
    )
    key_acc = lax.dynamic_update_slice_in_dim(
        key_acc,
        lax.dynamic_slice_in_dim(key_acc, window_start, window_rows, 0)
        + key_part.reshape(window_rows, head_cols),
        window_start,
        0,
    )
    value_acc = lax.dynamic_update_slice_in_dim(
        value_acc,
        lax.dynamic_slice_in_dim(value_acc, window_start, window_rows, 0)
        + value_part.reshape(window_rows, head_cols),
        window_start,
        0,
    )
    return ((key_acc, value_acc), query_grad.reshape(block_len, head_cols))


def contract_rows(left, right):
    return lax.dot_general(
        left, right, (((0,), (0,)), ((), ())), preferred_element_type=jnp.float32
    )


def contract_cols(left, right):
    return lax.dot_general(
        left, right, (((1,), (1,)), ((), ())), preferred_element_type=jnp.float32
    )


def local(
    tokens,
    item_lengths,
    w_query,
    b_query,
    w_key,
    w_value,
    b_value,
    w_out,
    b_out,
    gain_attn,
    shift_attn,
    w_up,
    b_up,
    w_down,
    b_down,
    gain_ffn,
    shift_ffn,
    out_grad,
):
    rows_here = tokens.shape[0]
    token_count = rows_here * lax.axis_size("narrow")
    block_rows = BLOCK
    block_count = token_count // block_rows
    block_start, block_length = item_layout(item_lengths, block_rows, block_count)
    full_tokens = lax.all_gather(tokens, "narrow", axis=0, tiled=True)
    head_cols = w_query.shape[1]
    joint_weight = jnp.concatenate([w_query, w_key, w_value], axis=1)
    joint_bias = jnp.concatenate(
        [
            b_query.astype(jnp.float32),
            jnp.zeros((head_cols,), jnp.float32),
            b_value.astype(jnp.float32),
        ]
    )
    projected = jnp.dot(full_tokens, joint_weight, preferred_element_type=jnp.float32) + joint_bias
    query_rows = projected[:, :head_cols].astype(jnp.bfloat16)
    key_rows = projected[:, head_cols : 2 * head_cols].astype(jnp.bfloat16)
    value_rows = projected[:, 2 * head_cols :].astype(jnp.bfloat16)
    query_blocks = query_rows.reshape(block_count, block_rows, head_cols)

    def attend(inputs):
        query_block, item_start, item_length = inputs
        window_start = jnp.minimum(item_start, token_count - 2 * block_rows)
        return forward_block(
            query_block, key_rows, value_rows, item_start, item_length, window_start, 2 * block_rows
        )

    context_blocks, log_totals = lax.map(attend, (query_blocks, block_start, block_length))
    context = context_blocks.reshape(token_count, head_cols)
    attn_sum = lax.psum_scatter(
        jnp.dot(context, w_out, preferred_element_type=jnp.float32).astype(jnp.bfloat16),
        "narrow",
        scatter_dimension=0,
        tiled=True,
    ).astype(jnp.float32)
    resid_one = tokens.astype(jnp.float32) + attn_sum + b_out.astype(jnp.float32)
    normed_one, unit_one, inv_one = layer_norm(resid_one, gain_attn, shift_attn)
    normed_low = normed_one.astype(jnp.bfloat16)
    full_normed = lax.all_gather(normed_low, "narrow", axis=0, tiled=True)
    pre_act = jnp.dot(full_normed, w_up, preferred_element_type=jnp.float32) + b_up.astype(
        jnp.float32
    )
    activated = jax.nn.gelu(pre_act, approximate=False).astype(jnp.bfloat16)
    ffn_sum = lax.psum_scatter(
        jnp.dot(activated, w_down, preferred_element_type=jnp.float32).astype(jnp.bfloat16),
        "narrow",
        scatter_dimension=0,
        tiled=True,
    ).astype(jnp.float32)
    resid_two = normed_one + ffn_sum + b_down.astype(jnp.float32)
    final_norm, unit_two, inv_two = layer_norm(resid_two, gain_ffn, shift_ffn)
    layer_out = final_norm.astype(jnp.bfloat16)
    resid_two_grad, gain_ffn_part, shift_ffn_part = norm_backward(
        out_grad.astype(jnp.float32), unit_two, inv_two, gain_ffn
    )
    ffn_grad_low = resid_two_grad.astype(jnp.bfloat16)
    b_down_part = jnp.sum(ffn_grad_low.astype(jnp.float32), axis=0)
    full_ffn_grad = lax.all_gather(ffn_grad_low, "narrow", axis=0, tiled=True)
    w_down_grad = contract_rows(activated, full_ffn_grad)
    pre_grad = (contract_cols(full_ffn_grad, w_down) * gelu_slope(pre_act)).astype(jnp.bfloat16)
    b_up_grad = jnp.sum(pre_grad.astype(jnp.float32), axis=0)
    w_up_grad = contract_rows(full_normed, pre_grad)
    normed_grad = resid_two_grad + lax.psum_scatter(
        contract_cols(pre_grad, w_up).astype(jnp.bfloat16),
        "narrow",
        scatter_dimension=0,
        tiled=True,
    ).astype(jnp.float32)
    resid_one_grad, gain_attn_part, shift_attn_part = norm_backward(
        normed_grad, unit_one, inv_one, gain_attn
    )
    attn_grad_low = resid_one_grad.astype(jnp.bfloat16)
    b_out_part = jnp.sum(attn_grad_low.astype(jnp.float32), axis=0)
    full_attn_grad = lax.all_gather(attn_grad_low, "narrow", axis=0, tiled=True)
    w_out_grad = contract_rows(context, full_attn_grad)
    context_grad = contract_cols(full_attn_grad, w_out).astype(jnp.bfloat16)
    grad_blocks = context_grad.reshape(block_count, block_rows, head_cols)

    def backward_step(running, inputs):
        query_block, grad_block, row_lse, item_start, item_length = inputs
        window_start = jnp.minimum(item_start, token_count - 2 * block_rows)
        return backward_block(
            running,
            query_block,
            grad_block,
            row_lse,
            item_start,
            item_length,
            key_rows,
            value_rows,
            window_start,
            2 * block_rows,
        )

    zero_acc = jnp.zeros((token_count, head_cols), jnp.float32)
    (key_acc, value_acc), query_grad_blocks = lax.scan(
        backward_step,
        (zero_acc, zero_acc),
        (query_blocks, grad_blocks, log_totals, block_start, block_length),
    )
    query_grad = query_grad_blocks.reshape(token_count, head_cols).astype(jnp.bfloat16)
    key_grad = key_acc.astype(jnp.bfloat16)
    value_grad = value_acc.astype(jnp.bfloat16)
    joint_grad = jnp.concatenate([query_grad, key_grad, value_grad], axis=1)
    stacked_grad = contract_rows(full_tokens, joint_grad)
    w_query_grad = stacked_grad[:, :head_cols]
    w_key_grad = stacked_grad[:, head_cols : 2 * head_cols]
    w_value_grad = stacked_grad[:, 2 * head_cols :]
    b_query_grad = jnp.sum(query_grad.astype(jnp.float32), axis=0)
    b_value_grad = jnp.sum(value_grad.astype(jnp.float32), axis=0)
    token_grad = resid_one_grad + lax.psum_scatter(
        contract_cols(joint_grad, joint_weight).astype(jnp.bfloat16),
        "narrow",
        scatter_dimension=0,
        tiled=True,
    ).astype(jnp.float32)
    (
        w_query_grad,
        b_query_grad,
        w_key_grad,
        w_value_grad,
        b_value_grad,
        w_out_grad,
        w_up_grad,
        b_up_grad,
        w_down_grad,
    ) = lax.psum(
        (
            w_query_grad,
            b_query_grad,
            w_key_grad,
            w_value_grad,
            b_value_grad,
            w_out_grad,
            w_up_grad,
            b_up_grad,
            w_down_grad,
        ),
        "wide",
    )
    b_out_grad, b_down_grad, gain_attn_grad, shift_attn_grad, gain_ffn_grad, shift_ffn_grad = (
        lax.psum(
            (
                b_out_part,
                b_down_part,
                gain_attn_part,
                shift_attn_part,
                gain_ffn_part,
                shift_ffn_part,
            ),
            ("wide", "narrow"),
        )
    )
    return (
        layer_out,
        token_grad,
        w_query_grad,
        b_query_grad,
        w_key_grad,
        w_value_grad,
        b_value_grad,
        w_out_grad,
        b_out_grad,
        gain_attn_grad,
        shift_attn_grad,
        w_up_grad,
        b_up_grad,
        w_down_grad,
        b_down_grad,
        gain_ffn_grad,
        shift_ffn_grad,
    )


def solution(mesh):
    placed = (
        P(("wide", "narrow"), None),
        P("wide"),
        P(None, "narrow"),
        P("narrow"),
        P(None, "narrow"),
        P(None, "narrow"),
        P("narrow"),
        P("narrow", None),
        P(),
        P(),
        P(),
        P(None, "narrow"),
        P("narrow"),
        P("narrow", None),
        P(),
        P(),
        P(),
        P(("wide", "narrow"), None),
    )
    return jax.shard_map(
        local,
        mesh=mesh,
        in_specs=placed,
        out_specs=(
            P(("wide", "narrow"), None),
            P(("wide", "narrow"), None),
            P(None, "narrow"),
            P("narrow"),
            P(None, "narrow"),
            P(None, "narrow"),
            P("narrow"),
            P("narrow", None),
            P(),
            P(),
            P(),
            P(None, "narrow"),
            P("narrow"),
            P("narrow", None),
            P(),
            P(),
            P(),
        ),
        check_vma=False,
    )
```

profile of v0, /device:TPU:0, one launch (start us, length us, event | category | flops | bytes accessed | tf_op | source)
XLA Modules:
  0.0 762.3 jit_solution(12942335243531143669)
XLA Ops:
  14.9 26.0 %all-gather.5.cloned.1.call-done = bf16[2048,768]{1,0:T(8,128)(2,1)} async-done(((bf16[512,768]{1,0:T(8,128)(2,1)}), bf16[2048,768]{1,0:T(8,128)(2,1)}) %all-gather.5.cloned.1.call-update) | async-done | bytes 3145744 | tf_op jit(solution)/shard_map/all_gather | solution.py:193
  40.9 3.9 fusion.31
  47.2 46.3 %while.26 = (s32[]{:T(128)}, bf16[4,512,192]{1,2,0:T(8,128)(2,1)S(1)}, f32[4,3,512]{2,1,0:T(4,128)}, s32[4]{0:T(128)S(1)}, bf16[2048,192]{0,1:T(8,128)(2,1)}, /*...) while((s32[]{:T(128)}, ...), condition=%wide.region_7.8_spmd, body=%wide.region_4.7_spmd.sunk | while | flops 421628416 | bytes 22468844 | solution.py:216
  94.6 2.7 convolution_convert_fusion.3
  98.0 37.5 %reduce-scatter.5.cloned.1.call-done = bf16[512,768]{1,0:T(8,128)(2,1)} async-done(((bf16[2048,768]{1,0:T(8,128)(2,1)}), bf16[512,768]{1,0:T(8,128)(2,1)}) %reduce-scatter.5.cloned.1.call-update) | async-done | bytes 786448 | tf_op jit(solution)/shard_map/reduce_scatter | solution.py:218
  140.6 28.1 %all-gather.7.cloned.1.call-done = bf16[2048,768]{1,0:T(8,128)(2,1)} async-done(((bf16[512,768]{1,0:T(8,128)(2,1)}), bf16[2048,768]{1,0:T(8,128)(2,1)}) %all-gather.7.cloned.1.call-update) | async-done | bytes 3145744 | tf_op jit(solution)/shard_map/all_gather | solution.py:227
  168.7 18.4 %multiply_convert_fusion.1 = (bf16[2048,768]{1,0:T(8,128)(2,1)S(1)}, f32[2048,768]{1,0:T(8,128)}, f32[2048,768]{1,0:T(8,128)}) fusion(f32[768]{0:T(1024)S(1)} %convert_element_type.150, bf16[2048,768]{1,0:T(8,128)(2,1)} %all-gather.7.cloned.1.call-done, bf16[768,768]{1,0:T(8,128)(2,1)S(1)} %copy-done), kind=kOutput, calls=%fused_computation.50 | convolution fusion | flops 2519728128 | bytes 20057088 | tf_op jit(solution)/shard_map/dot_general | solution.py:228
  188.8 3.9 convolution_convert_fusion.1
  196.7 34.1 %reduce-scatter.7.cloned.1.call-done = bf16[512,768]{1,0:T(8,128)(2,1)} async-done(((bf16[2048,768]{1,0:T(8,128)(2,1)}), bf16[512,768]{1,0:T(8,128)(2,1)}) %reduce-scatter.7.cloned.1.call-update) | async-done | bytes 786448 | tf_op jit(solution)/shard_map/reduce_scatter | solution.py:232
  234.5 2.9 convert_reduce_fusion.2
  237.7 28.5 %all-gather.9.cloned.1.call-done = bf16[2048,768]{1,0:T(8,128)(2,1)} async-done(((bf16[512,768]{1,0:T(8,128)(2,1)}), bf16[2048,768]{1,0:T(8,128)(2,1)}) %all-gather.9.cloned.1.call-update) | async-done | bytes 3145744 | tf_op jit(solution)/shard_map/all_gather | solution.py:246
  266.2 10.4 %convert_reduce_fusion = (f32[768]{0:T(1024)}, bf16[2048,768]{1,0:T(8,128)(2,1)S(1)}) fusion(f32[2048,768]{1,0:T(8,128)} %get-tuple-element.271, f32[768]{0:T(1024)} %copy-done.29, f32[2048,768]{1,0:T(8,128)} %get-tuple-element.255, bf16[2048,768]{1,0:T(8,128)(2,1)} %all-gather.9.cloned.1.call-done, bf16[768,768]{1,0:T(8,128)(2,1)} %param.35), kind=kOutput, calls=%fused_computation.49 | convolution fusion | flops 2433219840 | bytes 20060160 | tf_op jit(solution)/shard_map/dot_general | solution.py:163
  278.3 4.0 convolution_convert_fusion
  282.4 38.1 %reduce-scatter.9.cloned.1.call-done = bf16[512,768]{1,0:T(8,128)(2,1)} async-done(((bf16[2048,768]{1,0:T(8,128)(2,1)}), bf16[512,768]{1,0:T(8,128)(2,1)}) %reduce-scatter.9.cloned.1.call-update) | async-done | bytes 786448 | tf_op jit(solution)/shard_map/reduce_scatter | solution.py:251
  320.5 3.2 multiply_reduce_fusion.1
  323.7 4.2 convert_reduce_fusion.3
  328.2 28.4 %all-gather.11.cloned.1.call-done = bf16[2048,768]{1,0:T(8,128)(2,1)} async-done(((bf16[512,768]{1,0:T(8,128)(2,1)}), bf16[2048,768]{1,0:T(8,128)(2,1)}) %all-gather.11.cloned.1.call-update) | async-done | bytes 3145744 | tf_op jit(solution)/shard_map/all_gather | solution.py:262
  356.6 3.1 convolution_convert_fusion.4
  362.2 94.5 %while.27 = (s32[]{:T(128)}, f32[2048,192]{0,1:T(8,128)S(1)}, f32[2048,192]{0,1:T(8,128)}, bf16[4,512,192]{1,2,0:T(8,128)(2,1)}, s32[4]{0:T(128)S(1)}, /*index=5...) while((s32[]{:T(128)}, f32[2048,192]{0,1:T(8,128)S(1)}, ...), condition=%wide.region_21.22_spmd, body=%wide.region_19.21_spmd.sunk | while | flops 1031014912 | bytes 67877168 | solution.py:284
  381.5 4.6 dynamic_update_slice.30
  397.4 2.1 multiply_reduce_fusion.7
  404.2 2.3 dynamic_update_slice.29
  406.5 4.5 dynamic_update_slice.30
  429.9 3.9 dynamic_update_slice.30
  452.8 3.9 dynamic_update_slice.30
  458.6 4.1 convolution_convert_fusion.2
  463.0 7.1 fusion.52
  470.1 4.2 fusion.51
  480.2 42.3 %all-reduce = (f32[768]{0:T(1024)}, f32[768]{0:T(1024)}, f32[768]{0:T(1024)}, f32[768]{0:T(1024)}, f32[768]{0:T(1024)}, /*index=5*/f32[768]{0:T(1024)}) all-reduce(f32[768]{0:T(1024)S(1)} %copy-done.27, f32[768]{0:T(1024)S(1)} %copy-done.25, f32[768]{0:T(1024)S(1)} %copy-done.26, ...), channel_id=1, replica_groups=mesh['wide'=8,'narrow'=4] {'wide','narrow'}, use_global_device_ids=true, to_apply=%region_32.33 | all-reduce | flops 4608 | bytes 36864 | tf_op jit(solution)/shard_map/psum | solution.py:330
  523.9 23.8 %all-reduce.1 = (f32[192]{0:T(256)}, f32[192]{0:T(256)}, f32[768]{0:T(1024)}) all-reduce(f32[192]{0:T(256)S(1)} %convert_reduce_fusion.5, f32[192]{0:T(256)S(1)} %get-tuple-element.250, f32[768]{0:T(1024)S(1)} %copy-done.28), channel_id=1, replica_groups=mesh['wide'=8,'narrow'=4] {'wide'}, use_global_device_ids=true, to_apply=%region_25.26 | all-reduce | flops 1152 | bytes 9216 | tf_op jit(solution)/shard_map/psum | solution.py:315
  547.7 2.4 convert_add_fusion
  550.1 195.8 %all-reduce.5.cloned.1.call-done = (f32[768,192]{0,1:T(8,128)}, f32[768,192]{0,1:T(8,128)}, f32[768,192]{0,1:T(8,128)}, f32[192,768]{1,0:T(8,128)}, f32[768,768]{1,0:T(8,128)}, /*index=5*/f32[768,768]{1,0:T(8,128)}) async-done(((f32[768,192]{0,1:T(8,128)}, f32[768,192]{0,1:T(8,128)}, f32[768,192]{0,1:T(8,128)}, f32[192,768]{1,0:T(8,128)}, f32[768,768]{1,0:T(8,128)}, /*index=5*/f32[768,768]{1,0:T(8,128)}), ...) | async-done | bytes 7077904 | tf_op jit(solution)/shard_map/psum | solution.py:315
  (273 shorter events, 153.0 us)
Async XLA Ops:
  7.2 161.5 %copy-start = (bf16[768,768]{1,0:T(8,128)(2,1)S(1)}, bf16[768,768]{1,0:T(8,128)(2,1)}, u32[]{:S(2)}) copy-start(bf16[768,768]{1,0:T(8,128)(2,1)} %param.33) | copy-start | bytes 3538948
  7.2 33.7 %all-gather.5.cloned.1.call-start = ((), (), s32[]{:S(2)}) async-start(), calls=%async_computation.4 | async-start | bytes 3932160 | tf_op jit(solution)/shard_map/all_gather | solution.py:193
  7.9 127.6 %reduce-scatter.5.cloned.1.call-start = ((), (), s32[]{:S(2)}) async-start(), calls=%async_computation.5 | async-start | bytes 3932160 | tf_op jit(solution)/shard_map/reduce_scatter | solution.py:218
  14.9 29.9 %copy-start.17 = (bf16[768,576]{0,1:T(8,128)(2,1)}, bf16[768,576]{0,1:T(8,128)(2,1)S(1)}, u32[]{:S(2)}) copy-start(bf16[768,576]{0,1:T(8,128)(2,1)S(1)} %constant_dynamic-update-slice_fusion.2) | copy-start | bytes 2654212
  47.2 47.4 %copy-start.15 = (bf16[192,768]{1,0:T(8,128)(2,1)S(1)}, bf16[192,768]{1,0:T(8,128)(2,1)}, u32[]{:S(2)}) copy-start(bf16[192,768]{1,0:T(8,128)(2,1)} %param.29) | copy-start | bytes 884740
  93.5 3.8 copy-start.34
  93.5 3.8 copy-start.36
  97.3 38.2 %copy-start.2 = (bf16[512,768]{1,0:T(8,128)(2,1)S(1)}, bf16[512,768]{1,0:T(8,128)(2,1)}, u32[]{:S(2)}) copy-start(bf16[512,768]{1,0:T(8,128)(2,1)} %param.22) | copy-start | bytes 2359300
  97.4 71.3 %all-gather.7.cloned.1.call-start = ((), (), s32[]{:S(2)}) async-start(), calls=%async_computation.6 | async-start | bytes 3932160 | tf_op jit(solution)/shard_map/all_gather | solution.py:227
  98.0 42.0 %copy-start.20 = (f32[768]{0:T(1024)}, f32[768]{0:T(1024)S(1)}, u32[]{:S(2)}) copy-start(f32[768]{0:T(1024)S(1)} %convert_element_type.148) | copy-start | bytes 9220
  98.0 42.6 %copy-start.33 = (bf16[768]{0:T(1024)(128)(2,1)S(1)}, bf16[768]{0:T(1024)(128)(2,1)}, u32[]{:S(2)}) copy-start(bf16[768]{0:T(1024)(128)(2,1)} %param.34) | copy-start | bytes 4612
  135.5 3.1 copy-start.5
  140.0 90.9 %reduce-scatter.7.cloned.1.call-start = ((), (), s32[]{:S(2)}) async-start(), calls=%async_computation.7 | async-start | bytes 3932160 | tf_op jit(solution)/shard_map/reduce_scatter | solution.py:232
  140.6 46.5 %copy-start.29 = (f32[768]{0:T(1024)}, f32[768]{0:T(1024)S(1)}, u32[]{:S(2)}) copy-start(f32[768]{0:T(1024)S(1)} %convert_element_type.150) | copy-start | bytes 9220
  168.7 20.1 %copy-start.40 = (bf16[768,768]{1,0:T(8,128)(2,1)S(1)}, bf16[768,768]{1,0:T(8,128)(2,1)}, u32[]{:S(2)}) copy-start(bf16[768,768]{1,0:T(8,128)(2,1)} %param.35) | copy-start | bytes 3538948
  192.8 40.4 %copy-start.10 = (bf16[512,768]{1,0:T(8,128)(2,1)S(1)}, bf16[512,768]{1,0:T(8,128)(2,1)}, u32[]{:S(2)}) copy-start(bf16[512,768]{1,0:T(8,128)(2,1)} %param.39) | copy-start | bytes 2359300
  192.8 73.4 %all-gather.9.cloned.1.call-start = ((), (), s32[]{:S(2)}) async-start(), calls=%async_computation.8 | async-start | bytes 3932160 | tf_op jit(solution)/shard_map/all_gather | solution.py:246
  230.9 3.6 copy-start.21
  237.5 83.0 %reduce-scatter.9.cloned.1.call-start = ((), (), s32[]{:S(2)}) async-start(), calls=%async_computation.9 | async-start | bytes 3932160 | tf_op jit(solution)/shard_map/reduce_scatter | solution.py:251
  282.3 74.3 %all-gather.11.cloned.1.call-start = ((), (), s32[]{:S(2)}) async-start(), calls=%async_computation.10 | async-start | bytes 3932160 | tf_op jit(solution)/shard_map/all_gather | solution.py:262
  320.5 3.2 copy-start.11
  323.7 32.9 %copy-start.16 = (bf16[192,768]{1,0:T(8,128)(2,1)S(1)}, bf16[192,768]{1,0:T(8,128)(2,1)}, u32[]{:S(2)}) copy-start(bf16[192,768]{1,0:T(8,128)(2,1)} %param.29) | copy-start | bytes 884740
  327.9 219.7 %reduce-scatter.11.cloned.1.call-start = ((), (), s32[]{:S(2)}) async-start(), calls=%async_computation.11 | async-start | bytes 3932160 | tf_op jit(solution)/shard_map/reduce_scatter | solution.py:299
  462.7 283.2 %all-reduce.5.cloned.1.call-start = ((), (), s32[]{:S(2)}) async-start(), calls=%async_computation.12 | async-start | bytes 14155776 | tf_op jit(solution)/shard_map/psum | solution.py:315
  463.0 7.1 copy-start.39
  463.0 7.1 copy-start.43
  470.1 4.2 copy-start.38
  474.3 3.3 copy-start.9
  479.5 44.4 %copy-start.28 = (f32[768]{0:T(1024)S(1)}, f32[768]{0:T(1024)}, u32[]{:S(2)}) copy-start(f32[768]{0:T(1024)} %get-tuple-element.272) | copy-start | bytes 9220
  479.5 68.2 %copy-start.8 = (f32[512,768]{1,0:T(8,128)S(1)}, f32[512,768]{1,0:T(8,128)}, u32[]{:S(2)}) copy-start(f32[512,768]{1,0:T(8,128)} %get-tuple-element.249) | copy-start | bytes 4718596
  745.9 5.9 copy-start.14
  745.9 6.7 copy-start.13
  (24 other events, 35.3 us)
Sparse Core Ops, SparseCore 0:
  9.6 31.2 all-gather.4
  97.5 37.9 reduce-scatter.4
  140.1 28.5 all-gather.6
  192.9 37.9 reduce-scatter.6
  237.6 28.5 all-gather.8
  282.4 37.9 reduce-scatter.8
  328.1 28.5 all-gather.10
  462.8 38.8 reduce-scatter.10
  507.9 237.9 all-reduce.4
where the time goes:
time: 770 us; the launch traced here: 762 us
  waiting for transfers between devices  417 us (54%)
  matrix products  103 us (13%)
  local copies, waits for them, and re-layouts  90.4 us (12%)
  blocking collectives  66.1 us (9%)
  other arithmetic  53.2 us (7%)
  loops' own time  16.2 us (2%)
  between operations  14.5 us (2%)
    psum x1, waiting for transfers between devices, local(): lax.psum((w_query_grad, b_query_grad, w_key_grad, w_value_grad, b_value_g...  196 us
    psum x1, blocking collectives, local(): lax.psum((b_out_part, b_down_part, gain_attn_part, shift_attn_part, gain_...  42.3 us
    reduce_scatter x1, waiting for transfers between devices, local(): lax.psum_scatter(contract_cols(pre_grad, w_up).astype(jnp.bfloat16), 'nar...  38.1 us
    reduce_scatter x1, waiting for transfers between devices, local(): lax.psum_scatter(jnp.dot(context, w_out, preferred_element_type=jnp.float...  37.5 us
    reduce_scatter x1, waiting for transfers between devices, local(): lax.psum_scatter(jnp.dot(activated, w_down, preferred_element_type=jnp.fl...  34.1 us
    all_gather x1, waiting for transfers between devices, local(): full_ffn_grad = lax.all_gather(ffn_grad_low, 'narrow', axis=0, tiled=True)  28.5 us
    all_gather x1, waiting for transfers between devices, local(): full_attn_grad = lax.all_gather(attn_grad_low, 'narrow', axis=0, tiled=True)  28.4 us
    all_gather x1, waiting for transfers between devices, local(): full_normed = lax.all_gather(normed_low, 'narrow', axis=0, tiled=True)  28.1 us
  transfers between devices with their start and end apart: 9, of which 8 were waited for; matrix products, arithmetic and copies ran while one was open for 4% of the time, Pallas kernels for 0%

commit v1 on v0

v1 whole, which is shorter than its diff:
```python
import functools

import jax
import jax.numpy as jnp
from jax import lax
from jax.experimental import pallas as pl
from jax.experimental.pallas import tpu as pltpu
from jax.sharding import PartitionSpec as P

HD = 64
F32 = jnp.float32
BF = jnp.bfloat16
MIB = 1 << 20

norm_eps = 1e-12
masked_shift = 1e30
half_root = 0.7071067811865476
inv_root_two_pi = 0.3989422804014327
score_scale = HD**-0.5

VM = pl.BlockSpec(memory_space=pltpu.VMEM)
SM = pl.BlockSpec(memory_space=pltpu.SMEM)
ANY = pl.BlockSpec(memory_space=pl.ANY)


def dot(left, right):
    return jnp.dot(left, right, preferred_element_type=F32)


def contract_rows(left, right):
    return lax.dot_general(left, right, (((0,), (0,)), ((), ())), preferred_element_type=F32)


def contract_cols(left, right):
    return lax.dot_general(left, right, (((1,), (1,)), ((), ())), preferred_element_type=F32)


def shape(dims, dtype):
    return jax.ShapeDtypeStruct(dims, dtype)


def row(ref):
    return ref[...].astype(F32).reshape(1, -1)


def call(kernel, name, out_shape, args, smem=0, scratch=(), vmem=24, aliases=None, after=()):
    count = len(args)

    def body(*refs):
        kernel(*refs[:count], *refs[count + len(after) :])

    return pl.pallas_call(
        body,
        out_shape=tuple(out_shape),
        in_specs=[SM] * smem + [VM] * (count - smem) + [ANY] * len(after),
        out_specs=tuple([VM] * len(out_shape)),
        scratch_shapes=list(scratch),
        input_output_aliases=aliases or {},
        compiler_params=pltpu.CompilerParams(vmem_limit_bytes=vmem * MIB),
        cost_estimate=pl.CostEstimate(flops=1000, transcendentals=0, bytes_accessed=1000),
        name=name,
    )(*args, *after)


def joint_kernel(wq_ref, wk_ref, wv_ref, bq_ref, bv_ref, bu_ref, out_ref, tail_s):
    cols = wq_ref.shape[0]
    for i, ref in enumerate((wq_ref, wk_ref, wv_ref)):
        out_ref[i * cols : (i + 1) * cols] = ref[...]
    tail_s[...] = jnp.zeros_like(tail_s)
    tail_s[0:1, 0:cols] = row(bq_ref)
    tail_s[1:2, 0:cols] = row(bv_ref)
    tail_s[2:3, :] = row(bu_ref)
    out_ref[3 * cols : 3 * cols + 16] = tail_s[...].astype(BF)


def pack_joint(w_query, w_key, w_value, b_query, b_value, b_up):
    width, cols = w_query.shape
    return call(
        joint_kernel, "pack_joint", [shape((3 * cols + 16, width), BF)],
        (w_query.T, w_key.T, w_value.T, b_query, b_value, b_up),
        scratch=[pltpu.VMEM((16, width), F32)], vmem=8,
    )[0]


def neighbour(lens_ref, me_ref, rows):
    me = me_ref[0]
    here = me * rows
    first = jnp.int32(0)
    start = jnp.int32(0)
    length = jnp.int32(0)
    for j in range(lens_ref.shape[0]):
        n = lens_ref[j]
        inside = (first <= here) & (here < first + n)
        start = jnp.where(inside, first, start)
        length = jnp.where(inside, n, length)
        first = first + n
    other = jnp.where(start == here, me + 1, me - 1)
    return length > rows, other == (me ^ 1)


def pick_other(use_core, core_ref, mid_ref, out_s):
    @pl.when(use_core)
    def _():
        out_s[...] = core_ref[...]

    @pl.when(jnp.logical_not(use_core))
    def _():
        out_s[...] = mid_ref[...]


def attend_kernel(
    lens_ref, me_ref, own_ref, core_ref, mid_ref, a_ref,
    ctx_ref, lse_ref, q_ref, k_ref, v_ref,
    oth_s, qt_s, vt_s, ct_s, *, tile,
):
    rows = own_ref.shape[0]
    cols = q_ref.shape[1]
    flag, use_core = neighbour(lens_ref, me_ref, rows)
    pick_other(use_core, core_ref, mid_ref, oth_s)
    tail = a_ref[3 * cols : 3 * cols + 16].astype(F32)
    wk = a_ref[cols : 2 * cols]
    wv = a_ref[2 * cols : 3 * cols]
    own = own_ref[...]
    q = (contract_cols(own, a_ref[0:cols]) + tail[0:1, 0:cols]).astype(BF)
    q = q * jnp.asarray(score_scale, BF)
    q_ref[...] = q
    qt_s[...] = q.T
    k_ref[0:rows] = contract_cols(own, wk).astype(BF)
    v_own = (contract_cols(own, wv) + tail[1:2, 0:cols]).astype(BF)
    v_ref[0:rows] = v_own
    vt_s[:, 0:rows] = v_own.T
    other = oth_s[...]
    k_ref[rows : 2 * rows] = contract_cols(other, wk).astype(BF)
    v_other = (contract_cols(other, wv) + tail[1:2, 0:cols]).astype(BF)
    v_ref[rows : 2 * rows] = v_other
    vt_s[:, rows : 2 * rows] = v_other.T
    for h in range(cols // HD):
        hs = slice(h * HD, (h + 1) * HD)
        for t in range(rows // tile):
            ts = slice(t * tile, (t + 1) * tile)
            q_h = qt_s[hs, ts]
            s_own = dot(k_ref[0:rows, hs], q_h)
            s_other = dot(k_ref[rows : 2 * rows, hs], q_h)
            top_own = jnp.max(s_own, axis=0, keepdims=True)
            top_other = jnp.max(s_other, axis=0, keepdims=True)
            top = jnp.where(flag, jnp.maximum(top_own, top_other), top_own)
            p_own = jnp.exp(s_own - top)
            p_other = jnp.exp(s_other - jnp.where(flag, top, masked_shift))
            total = jnp.sum(p_own, axis=0, keepdims=True) + jnp.sum(p_other, axis=0, keepdims=True)
            c = dot(vt_s[hs, 0:rows], p_own.astype(BF)) + dot(
                vt_s[hs, rows : 2 * rows], p_other.astype(BF)
            )
            ct_s[hs, ts] = c * (1.0 / total)
            lse_ref[h : h + 1, ts] = top + jnp.log(total)
    ctx_ref[...] = ct_s[...].T.astype(BF)


def attend(lens, me, own, tok_core, tok_mid, a, after=(), tile=256):
    rows, width = own.shape
    cols = (a.shape[0] - 16) // 3
    return call(
        functools.partial(attend_kernel, tile=tile), "attend",
        [
            shape((rows, cols), BF), shape((cols // HD, rows), F32), shape((rows, cols), BF),
            shape((2 * rows, cols), BF), shape((2 * rows, cols), BF),
        ],
        (lens, me, own, tok_core, tok_mid, a), smem=2, after=after,
        scratch=[
            pltpu.VMEM((rows, width), BF), pltpu.VMEM((cols, rows), BF),
            pltpu.VMEM((cols, 2 * rows), BF), pltpu.VMEM((cols, rows), F32),
        ],
    )


def attend_back_kernel(
    lens_ref, me_ref, own_ref, core_ref, mid_ref, a_ref, wo_ref, g_ref,
    ctx_ref, lse_ref, q_ref, k_ref, v_ref, tok_in_ref, oth_in_ref,
    qk_ref, vo_ref, tok_ref, oth_ref, bq_ref, bv_ref,
    oth_s, gt_s, qt_s, kt_s, dqt_s, dk_s, dv_s, *, tile,
):
    rows, cols = q_ref.shape
    flag, use_core = neighbour(lens_ref, me_ref, rows)
    pick_other(use_core, core_ref, mid_ref, oth_s)
    attn_grad = g_ref[...]
    g = contract_cols(attn_grad, wo_ref[...]).astype(BF)
    gt_s[...] = g.T
    q = q_ref[...]
    qt_s[...] = q.T
    kt_s[...] = k_ref[...].T
    own = slice(0, rows)
    other = slice(rows, 2 * rows)
    for h in range(cols // HD):
        hs = slice(h * HD, (h + 1) * HD)
        for t in range(rows // tile):
            ts = slice(t * tile, (t + 1) * tile)
            q_h = qt_s[hs, ts]
            g_h = gt_s[hs, ts]
            lse = lse_ref[h : h + 1, ts]
            p_own = jnp.exp(dot(k_ref[own, hs], q_h) - lse)
            p_other = jnp.exp(dot(k_ref[other, hs], q_h) - jnp.where(flag, lse, masked_shift))
            dp_own = dot(v_ref[own, hs], g_h)
            dp_other = dot(v_ref[other, hs], g_h)
            row_dot = jnp.sum(p_own * dp_own, axis=0, keepdims=True) + jnp.sum(
                p_other * dp_other, axis=0, keepdims=True
            )
            ds_own = (p_own * (dp_own - row_dot)).astype(BF)
            ds_other = (p_other * (dp_other - row_dot)).astype(BF)
            dqt_s[hs, ts] = dot(kt_s[hs, own], ds_own) + dot(kt_s[hs, other], ds_other)
            q_n = q[ts, hs]
            g_n = g[ts, hs]
            parts = (
                dot(ds_own, q_n), dot(ds_other, q_n),
                dot(p_own.astype(BF), g_n), dot(p_other.astype(BF), g_n),
            )
            if t == 0:
                dk_s[own, hs], dk_s[other, hs], dv_s[own, hs], dv_s[other, hs] = parts
            else:
                dk_s[own, hs] += parts[0]
                dk_s[other, hs] += parts[1]
                dv_s[own, hs] += parts[2]
                dv_s[other, hs] += parts[3]
    dqt = (dqt_s[...] * score_scale).astype(BF)
    dq = dqt.T
    dk = dk_s[...].astype(BF)
    dv = dv_s[...].astype(BF)
    dkt = dk.T
    dvt = dv.T
    tok = own_ref[...]
    oth = oth_s[...]
    qk_ref[0:cols] = dot(dqt, tok).astype(BF)
    qk_ref[cols : 2 * cols] = (dot(dkt[:, own], tok) + dot(dkt[:, other], oth)).astype(BF)
    vo_ref[0:cols] = (dot(dvt[:, own], tok) + dot(dvt[:, other], oth)).astype(BF)
    vo_ref[cols : 2 * cols] = contract_rows(ctx_ref[...], attn_grad).astype(BF)
    wq = a_ref[0:cols]
    wk = a_ref[cols : 2 * cols]
    wv = a_ref[2 * cols : 3 * cols]
    tok_ref[...] = tok_in_ref[...] + dot(dq, wq) + dot(dk[own], wk) + dot(dv[own], wv)
    oth_ref[...] = oth_in_ref[...] + dot(dk[other], wk) + dot(dv[other], wv)
    bq_ref[...] = jnp.sum(dq.astype(F32), axis=0, keepdims=True)
    bv_ref[...] = jnp.sum(dv.astype(F32), axis=0, keepdims=True)


def attend_back(
    lens, me, own, tok_core, tok_mid, a, w_out, attn_grad, saved, tok_acc, oth_acc, after=(), tile=256
):
    rows, width = own.shape
    ctx, lse, q, k, v = saved
    cols = q.shape[1]
    return call(
        functools.partial(attend_back_kernel, tile=tile), "attend_back",
        [
            shape((2 * cols, width), BF), shape((2 * cols, width), BF),
            shape((rows, width), F32), shape((rows, width), F32),
            shape((1, cols), F32), shape((1, cols), F32),
        ],
        (
            lens, me, own, tok_core, tok_mid, a, w_out, attn_grad, ctx, lse, q, k, v,
            tok_acc, oth_acc,
        ),
        smem=2,
        scratch=[
            pltpu.VMEM((rows, width), BF),
            pltpu.VMEM((cols, rows), BF), pltpu.VMEM((cols, rows), BF),
            pltpu.VMEM((cols, 2 * rows), BF), pltpu.VMEM((cols, rows), F32),
            pltpu.VMEM((2 * rows, cols), F32), pltpu.VMEM((2 * rows, cols), F32),
        ],
        vmem=32,
        aliases={13: 2, 14: 3}, after=after,
    )


def unit_of(residual):
    centre = jnp.mean(residual, axis=1, keepdims=True)
    spread = residual - centre
    inverse = lax.rsqrt(jnp.mean(spread * spread, axis=1, keepdims=True) + norm_eps)
    return spread * inverse, inverse


def norm_back(upstream, unit_rows, inverse, gain):
    unit_grad = upstream * gain
    return inverse * (
        unit_grad
        - jnp.mean(unit_grad, axis=1, keepdims=True)
        - unit_rows * jnp.mean(unit_grad * unit_rows, axis=1, keepdims=True)
    )


def first_norm_kernel(
    tok_ref, c0_ref, c1_ref, c2_ref, c3_ref, a0_ref, a1_ref, a2_ref, a3_ref,
    bo_ref, gain_ref, shift_ref, unit_ref, inv_ref, low_ref,
):
    resid = tok_ref[...].astype(F32) + row(bo_ref)
    for c_ref, a_ref in ((c0_ref, a0_ref), (c1_ref, a1_ref), (c2_ref, a2_ref), (c3_ref, a3_ref)):
        resid = resid + dot(c_ref[...], a_ref[...])
    unit, inverse = unit_of(resid)
    unit_ref[...] = unit
    inv_ref[...] = inverse
    low_ref[...] = (unit * row(gain_ref) + row(shift_ref)).astype(BF)


def first_norm(tokens, ctxs, outs, b_out, gain, shift, after=()):
    rows, width = tokens.shape
    return call(
        first_norm_kernel, "first_norm",
        [shape((rows, width), F32), shape((rows, 1), F32), shape((rows, width), BF)],
        (tokens, *ctxs, *outs, b_out, gain, shift), after=after,
    )


def up_down(low_ref, a_ref, up_refs, down_ref, act_ref, slope_ref):
    units = act_ref.shape[1]
    at = a_ref.shape[0] - 16
    bias = a_ref[at : at + 16].astype(F32)[2:3]
    step = 256
    for c in range(units // step):
        cs = slice(c * step, (c + 1) * step)
        pre = bias[:, cs]
        at = 0
        for up_ref in up_refs:
            depth = up_ref.shape[0]
            pre = pre + dot(low_ref[:, at : at + depth], up_ref[:, cs])
            at += depth
        phi = 0.5 + 0.5 * lax.erf(pre * half_root)
        act_ref[:, cs] = (pre * phi).astype(BF)
        slope_ref[:, cs] = (phi + pre * jnp.exp(-0.5 * pre * pre) * inv_root_two_pi).astype(BF)
    return dot(act_ref[...], down_ref[...])


def ffn_near_kernel(
    low_ref, a0_ref, a1_ref, u0_ref, u1_ref, d0_ref, d1_ref,
    act0_ref, act1_ref, sl0_ref, sl1_ref, sum_ref,
):
    part = up_down(low_ref, a0_ref, (u0_ref,), d0_ref, act0_ref, sl0_ref)
    sum_ref[...] = part + up_down(low_ref, a1_ref, (u1_ref,), d1_ref, act1_ref, sl1_ref)


def ffn_near(low, joints, ups, downs, after=()):
    rows, width = low.shape
    units = ups[0].shape[1]
    piece = shape((rows, units), BF)
    return call(
        ffn_near_kernel, "ffn_near", [piece, piece, piece, piece, shape((rows, width), F32)],
        (low, *joints, *ups, *downs), after=after,
        vmem=32,
    )


def ffn_far_kernel(
    low_ref, a0_ref, a1_ref, u0a_ref, u0b_ref, u1a_ref, u1b_ref, d0_ref, d1_ref,
    unit_ref, sum_ref, out_grad_ref, gain1_ref, shift1_ref, bd_ref, gain2_ref, shift2_ref,
    act0_ref, act1_ref, sl0_ref, sl1_ref, out_ref, resid_ref, low_grad_ref,
    bd_out, gain_out, shift_out,
):
    part = sum_ref[...] + up_down(low_ref, a0_ref, (u0a_ref, u0b_ref), d0_ref, act0_ref, sl0_ref)
    part = part + up_down(low_ref, a1_ref, (u1a_ref, u1b_ref), d1_ref, act1_ref, sl1_ref)
    resid = unit_ref[...] * row(gain1_ref) + (row(shift1_ref) + row(bd_ref)) + part
    unit, inverse = unit_of(resid)
    gain = row(gain2_ref)
    out_ref[...] = (unit * gain + row(shift2_ref)).astype(BF)
    upstream = out_grad_ref[...].astype(F32)
    gain_out[...] = jnp.sum(upstream * unit, axis=0, keepdims=True)
    shift_out[...] = jnp.sum(upstream, axis=0, keepdims=True)
    back = norm_back(upstream, unit, inverse, gain)
    resid_ref[...] = back
    low_grad = back.astype(BF)
    low_grad_ref[...] = low_grad
    bd_out[...] = jnp.sum(low_grad.astype(F32), axis=0, keepdims=True)


def ffn_far(
    low, joints, ups, downs, unit, near_sum, out_grad, gain1, shift1, b_down, gain2, shift2, after=()
):
    rows, width = low.shape
    units = downs[0].shape[0]
    piece = shape((rows, units), BF)
    vec = shape((1, width), F32)
    return call(
        ffn_far_kernel, "ffn_far",
        [
            piece, piece, piece, piece,
            shape((rows, width), BF), shape((rows, width), F32), shape((rows, width), BF),
            vec, vec, vec,
        ],
        (
            low, *joints, *ups[0], *ups[1], *downs, unit, near_sum, out_grad,
            gain1, shift1, b_down, gain2, shift2,
        ),
        after=after,
        vmem=40,
    )


def ffn_back_kernel(g_ref, low_ref, act_ref, slope_ref, sum_in_ref, down_ref, *refs):
    up_refs = refs[:-5]
    down_grad_ref, up_grad_ref, bias_ref, sum_ref, pre_s = refs[-5:]
    g = g_ref[...]
    units = down_ref.shape[0]
    down_grad_ref[...] = contract_rows(act_ref[...], g).astype(BF)
    step = 256
    for c in range(units // step):
        cs = slice(c * step, (c + 1) * step)
        pre = (contract_cols(g, down_ref[cs]) * slope_ref[:, cs].astype(F32)).astype(BF)
        pre_s[:, cs] = pre
        bias_ref[:, cs] = jnp.sum(pre.astype(F32), axis=0, keepdims=True)
    pre = pre_s[...]
    up_grad_ref[...] = contract_rows(low_ref[...], pre).astype(BF)
    at = 0
    for up_ref in up_refs:
        cs = slice(at, at + up_ref.shape[0])
        sum_ref[:, cs] = sum_in_ref[:, cs] + contract_cols(pre, up_ref[...])
        at += up_ref.shape[0]


def ffn_back(g, low, act, slope, up, down, acc, after=()):
    rows, width = low.shape
    units = down.shape[0]
    return call(
        ffn_back_kernel, "ffn_back",
        [
            shape((units, width), BF), shape((width, units), BF),
            shape((1, units), F32), shape((rows, width), F32),
        ],
        (g, low, act, slope, acc, down, *up), after=after,
        scratch=[pltpu.VMEM((rows, units), BF)],
        aliases={4: 3}, vmem=32,
    )


def first_norm_back_kernel(
    up_ref, unit_ref, inv_ref, gain_ref, resid_ref, low_ref, bo_out, gain_out, shift_out
):
    upstream = up_ref[...]
    unit = unit_ref[...]
    gain_out[...] = jnp.sum(upstream * unit, axis=0, keepdims=True)
    shift_out[...] = jnp.sum(upstream, axis=0, keepdims=True)
    back = norm_back(upstream, unit, inv_ref[...], row(gain_ref))
    resid_ref[...] = back
    low = back.astype(BF)
    low_ref[...] = low
    bo_out[...] = jnp.sum(low.astype(F32), axis=0, keepdims=True)


def first_norm_back(upstream, unit, inverse, gain, after=()):
    rows, width = unit.shape
    vec = shape((1, width), F32)
    return call(
        first_norm_back_kernel, "first_norm_back",
        [shape((rows, width), F32), shape((rows, width), BF), vec, vec, vec],
        (upstream, unit, inverse, gain), after=after,
    )


def gather_small_kernel(me_ref, *refs):
    out_ref = refs[-1]
    bq, bv, bu, rest = refs[0:4], refs[4:8], refs[8:12], refs[12:18]
    out_ref[...] = jnp.zeros_like(out_ref)
    cols = bq[0].shape[1]
    for r in range(4):
        at = 3 * (me_ref[0] ^ r)
        out_ref[pl.ds(at, 1), 0:cols] = bq[r][...]
        out_ref[pl.ds(at + 1, 1), 0:cols] = bv[r][...]
        out_ref[pl.ds(at + 2, 1), :] = bu[r][...]
    for i, ref in enumerate(rest):
        out_ref[12 + i : 13 + i, :] = ref[...]


def gather_small(me, bq, bv, bu, rest):
    width = rest[0].shape[1]
    return call(
        gather_small_kernel, "gather_small", [shape((24, width), F32)],
        (me, *bq, *bv, *bu, *rest), smem=1, vmem=4,
    )[0]


def spread_small_kernel(me_ref, in_ref, bq_ref, bv_ref, bu_ref, *rest):
    cols = bq_ref.shape[0]
    at = 3 * me_ref[0]
    bq_ref[...] = in_ref[pl.ds(at, 1), 0:cols].reshape(cols)
    bv_ref[...] = in_ref[pl.ds(at + 1, 1), 0:cols].reshape(cols)
    bu_ref[...] = in_ref[pl.ds(at + 2, 1), :].reshape(-1)
    for i, ref in enumerate(rest):
        ref[...] = in_ref[12 + i : 13 + i, :].reshape(-1)


def spread_small(me, sums, cols, units):
    width = sums.shape[1]
    return call(
        spread_small_kernel, "spread_small",
        [shape((cols,), F32), shape((cols,), F32), shape((units,), F32)] + [shape((width,), F32)] * 6,
        (me, sums), smem=1, vmem=4,
    )


def swap(a, axis, distance):
    size = lax.axis_size(axis)
    return lax.ppermute(a, axis, [(i, i ^ distance) for i in range(size)])


def to_core(a):
    return swap(a, "narrow", 1)


def to_chip(a):
    return swap(a, "narrow", 2)


def to_middle(a):
    return lax.ppermute(a, "narrow", [(1, 2), (2, 1)])


def wide_bits():
    size = lax.axis_size("wide")
    bits = []
    while size > 1:
        assert size % 2 == 0
        bits.append(len(bits))
        size //= 2
    return bits


def sum_small(a):
    for distance in (1, 2):
        a = a + swap(a, "narrow", distance)
    for bit in wide_bits():
        a = a + swap(a, "wide", 1 << bit)
    return a


def half_of(a, which):
    rows = a.shape[0] // 2
    return lax.dynamic_slice_in_dim(a, which * rows, rows, 0)


def side_of(bit):
    return (lax.axis_index("wide") >> bit) & 1


def in_order(side, mine, got):
    return jnp.where(side == 0, jnp.concatenate([mine, got]), jnp.concatenate([got, mine]))


def hold(a, *others):
    return lax.optimization_barrier((a, *others))[0]


def gather_wide(piece, waits=()):
    got = None
    for i, bit in enumerate(reversed(wide_bits())):
        got = swap(piece, "wide", 1 << bit)
        if i < len(waits) and waits[i] is not None:
            got = hold(got, waits[i])
        piece = in_order(side_of(bit), piece, got)
    return piece


def own_piece(a):
    rows = a.shape[0] // lax.axis_size("wide")
    at = 0
    for bit in wide_bits():
        at = 2 * at + side_of(bit)
    return lax.dynamic_slice_in_dim(a, at * rows, rows, 0)


def add_low(*terms):
    total = terms[0].astype(F32)
    for term in terms[1:]:
        total = total + term.astype(F32)
    return total.astype(BF)


def halve(a, bit):
    side = side_of(bit)
    return half_of(a, 1 - side), half_of(a, side)


class Scatter:
    def __init__(self, a):
        self.bits = wide_bits()
        self.a = a
        self.got = []
        self.step = 0
        self.send()

    def send(self):
        bit = self.bits[self.step]
        if bit < 3:
            out, self.keep = halve(self.a, bit)
        else:
            out, self.keep = self.a, self.a
        self.got.append(swap(out, "wide", 1 << bit))

    def advance(self, *waits):
        got = hold(self.got[-1], *waits) if waits else self.got[-1]
        self.a = add_low(self.keep, got)
        self.step += 1
        if self.step < len(self.bits):
            self.send()
            return False
        return True

    def finish(self):
        while self.step < len(self.bits):
            self.advance()
        return self.a


def gather_halves(a):
    for bit in reversed(wide_bits()[:3]):
        a = in_order(side_of(bit), a, swap(a, "wide", 1 << bit))
    return a.astype(F32)


def local(
    tokens, item_lengths, w_query, b_query, w_key, w_value, b_value, w_out, b_out,
    gain_attn, shift_attn, w_up, b_up, w_down, b_down, gain_ffn, shift_ffn, out_grad,
):
    rows, width = tokens.shape
    cols = w_query.shape[1]
    units = w_up.shape[1]
    assert lax.axis_size("narrow") == 4
    me = lax.axis_index("narrow").reshape(1)

    half = width // 2
    up_low, up_high = w_up[:half], w_up[half:]
    down_piece = to_chip(own_piece(w_down))
    high_piece = to_chip(own_piece(up_high))
    tok_mid = to_middle(tokens)
    tok_core = to_core(tokens)
    joint = pack_joint(w_query, w_key, w_value, b_query, b_value, b_up)
    joint_core = to_core(joint)
    joint_chip = to_chip(joint)

    saved = []

    def forward(r, block, *after):
        saved.append(attend(item_lengths, me, tokens, tok_core, tok_mid, block, after))
        return saved[-1][1]

    mark0 = forward(0, joint)
    out_chip = to_chip(hold(w_out, mark0))
    out_core = to_core(hold(w_out, mark0))
    mark1 = forward(1, joint_core, mark0)
    joint_diag = to_core(hold(joint_chip, mark1))
    low_chip = to_chip(hold(up_low, mark1))
    up_core = to_core(hold(w_up, mark1))
    down_chip = gather_wide(down_piece, (None, mark0, mark1))
    high_chip = gather_wide(high_piece, (None, mark0, mark1))
    mark2 = forward(2, joint_chip, mark1)
    out_diag = to_core(hold(out_chip, mark2))
    down_core = to_core(hold(w_down, mark2))
    mark3 = forward(3, joint_diag, mark2)
    down_diag = to_core(hold(down_chip, mark2))
    high_diag = to_core(hold(high_chip, mark3))
    low_diag = to_core(hold(low_chip, mark3))
    joints = [joint, joint_core, joint_chip, joint_diag]
    outs = [w_out, out_core, out_chip, out_diag]
    downs = [w_down, down_core, down_chip, down_diag]
    ups = [(w_up,), (up_core,), (low_chip, high_chip), (low_diag, high_diag)]

    unit_one, inv_one, low = first_norm(
        tokens, [s[0] for s in saved], outs, b_out, gain_attn, shift_attn
    )
    act0, act1, sl0, sl1, near = ffn_near(low, joints[:2], [w_up, up_core], downs[:2])
    (
        act2, act3, sl2, sl3, layer_out, resid_two, ffn_grad, b_down_part, gain_ffn_part,
        shift_ffn_part,
    ) = ffn_far(
        low, joints[2:], ups[2:], downs[2:], unit_one, near, out_grad,
        gain_attn, shift_attn, b_down, gain_ffn, shift_ffn,
    )
    acts = (act0, act1, act2, act3)
    slopes = (sl0, sl1, sl2, sl3)

    acc = resid_two
    down_parts, up_parts, bu_parts = [None] * 4, [None] * 4, [None] * 4

    def back(r, *after):
        nonlocal acc
        down_parts[r], up_parts[r], bu_parts[r], acc = ffn_back(
            ffn_grad, low, acts[r], slopes[r], ups[r], downs[r], acc, after
        )

    back(3)
    up_diag_sum = to_core(up_parts[3])
    down_diag_sum = to_core(down_parts[3])
    back(2)
    back(1, up_diag_sum, down_diag_sum)
    up_to_chip = to_chip(add_low(up_parts[2], up_diag_sum))
    far_down = Scatter(add_low(down_parts[2], down_diag_sum))
    down_core_sum = to_core(down_parts[1])
    up_core_sum = to_core(up_parts[1])
    back(0)

    resid_one, attn_grad, b_out_part, gain_attn_part, shift_attn_part = first_norm_back(
        acc, unit_one, inv_one, gain_attn, (down_core_sum,)
    )
    near_down = Scatter(add_low(down_parts[0], down_core_sum))
    tok_acc = resid_one
    oth_acc = jnp.zeros((rows, width), F32)
    qk_parts, vo_parts, bq_parts, bv_parts = [None] * 4, [None] * 4, [None] * 4, [None] * 4

    def back_attend(r, *after):
        nonlocal tok_acc, oth_acc
        qk_parts[r], vo_parts[r], tok_acc, oth_acc, bq_parts[r], bv_parts[r] = attend_back(
            item_lengths, me, tokens, tok_core, tok_mid, joints[r], outs[r], attn_grad, saved[r],
            tok_acc, oth_acc, after,
        )

    back_attend(3, up_core_sum)
    qk_diag = to_core(qk_parts[3])
    vo_diag = to_core(vo_parts[3])
    far_down.advance()
    back_attend(2, far_down.got[0])
    near_down.advance(bq_parts[2])
    far_down.advance(bq_parts[2])
    near_up = Scatter(add_low(up_parts[0], up_core_sum, hold(up_to_chip, bq_parts[2])))
    back_attend(1, near_down.got[0], far_down.got[1], up_to_chip, qk_diag, vo_diag)
    qk_to_chip = to_chip(add_low(qk_parts[2], qk_diag))
    vo_to_chip = to_chip(add_low(vo_parts[2], vo_diag))
    qk_core = to_core(qk_parts[1])
    vo_core = to_core(vo_parts[1])
    back_attend(0, near_down.got[1], far_down.got[2])
    far_piece = to_chip(far_down.finish())
    near_qk = Scatter(add_low(qk_parts[0], qk_core, qk_to_chip))
    near_vo = Scatter(add_low(vo_parts[0], vo_core, vo_to_chip))
    w_down_grad = gather_halves(add_low(near_down.finish(), far_piece))
    w_up_grad = gather_halves(near_up.finish())
    qk_grad = gather_halves(near_qk.finish())
    vo_grad = gather_halves(near_vo.finish())
    oth_low = oth_acc.astype(BF)
    token_grad = take_back(item_lengths, me, tok_acc, to_core(oth_low), to_middle(oth_low))

    small = gather_small(
        me, bq_parts, bv_parts, bu_parts,
        (b_out_part, b_down_part, gain_attn_part, shift_attn_part, gain_ffn_part, shift_ffn_part),
    )
    bq, bv, bu, b_out_g, b_down_g, gain_attn_g, shift_attn_g, gain_ffn_g, shift_ffn_g = spread_small(
        me, sum_small(small), cols, units
    )
    return (
        layer_out,
        token_grad,
        qk_grad[:cols].T,
        bq,
        qk_grad[cols:].T,
        vo_grad[:cols].T,
        bv,
        vo_grad[cols:],
        b_out_g,
        gain_attn_g,
        shift_attn_g,
        w_up_grad,
        bu,
        w_down_grad,
        b_down_g,
        gain_ffn_g,
        shift_ffn_g,
    )


def take_back_kernel(lens_ref, me_ref, tok_ref, core_ref, mid_ref, out_ref):
    flag, use_core = neighbour(lens_ref, me_ref, tok_ref.shape[0])

    @pl.when(jnp.logical_not(flag))
    def _():
        out_ref[...] = tok_ref[...]

    @pl.when(flag & use_core)
    def _():
        out_ref[...] = tok_ref[...] + core_ref[...].astype(F32)

    @pl.when(flag & jnp.logical_not(use_core))
    def _():
        out_ref[...] = tok_ref[...] + mid_ref[...].astype(F32)


def take_back(lens, me, tok_acc, core, mid):
    return call(
        take_back_kernel, "take_back", [shape(tok_acc.shape, F32)],
        (lens, me, tok_acc, core, mid), smem=2, vmem=12,
    )[0]


def solution(mesh):
    rows_spec = P(("wide", "narrow"), None)
    col_spec = P(None, "narrow")
    vec_spec = P("narrow")
    row_spec = P("narrow", None)
    full = P()
    return jax.shard_map(
        local,
        mesh=mesh,
        in_specs=(
            rows_spec, P("wide"), col_spec, vec_spec, col_spec, col_spec, vec_spec, row_spec, full,
            full, full, col_spec, vec_spec, row_spec, full, full, full, rows_spec,
        ),
        out_specs=(
            rows_spec, rows_spec, col_spec, vec_spec, col_spec, col_spec, vec_spec, row_spec, full,
            full, full, col_spec, vec_spec, row_spec, full, full, full,
        ),
        check_vma=False,
    )
```

time: 770 us -> 344 us (0.45)
  waiting for transfers between devices: 417 us -> 107 us
  Pallas kernels: 0 us -> 112 us
  matrix products: 103 us -> 0 us
  blocking collectives: 66.1 us -> 0 us
  starting transfers between devices: 1.53 us -> 50.9 us
  local copies, waits for them, and re-layouts: 90.4 us -> 41.9 us
  other arithmetic: 53.2 us -> 25.4 us
  loops' own time: 16.2 us -> 0 us
  between operations: 14.5 us -> 2.33 us
    psum x1 -> x0, waiting for transfers between devices: 196 us -> none  [local(): lax.psum((w_query_grad, b_query_grad, w_key_grad, w_value_grad, b_value_g...]
    pallas_call x0 -> x20, Pallas kernels: none -> 112 us  [call(): pl.pallas_call(body, out_shape=tuple(out_shape), in_specs=[SM] * smem + [...]
    all_gather x4 -> x0, waiting for transfers between devices: 111 us -> none  [the longest x1 28.5 us: local(): full_ffn_grad = lax.all_gather(ffn_grad_low, 'narrow', axis=0, tiled=True)]
    reduce_scatter x4 -> x0, waiting for transfers between devices: 110 us -> none  [the longest x1 38.1 us: local(): lax.psum_scatter(contract_cols(pre_grad, w_up).astype(jnp.bfloat16), 'nar...]
    ppermute x0 -> x68, waiting for transfers between devices: none -> 107 us  [the longest x66 107 us: swap(): return lax.ppermute(a, axis, [(i, i ^ distance) for i in range(size)])]
    dot_general x40 -> x0, matrix products: 103 us -> none  [the longest x4 21.6 us: contract_cols(): lax.dot_general(left, right, (((1,), (1,)), ((), ())), preferred_element_...]
    psum x2 -> x0, blocking collectives: 66.1 us -> none  [the longest x1 42.3 us: local(): lax.psum((b_out_part, b_down_part, gain_attn_part, shift_attn_part, gain_...]
    ppermute x0 -> x68, starting transfers between devices: none -> 50.9 us  [the longest x66 49.3 us: swap(): return lax.ppermute(a, axis, [(i, i ^ distance) for i in range(size)])]
  transfers between devices with their start and end apart: 9 -> 68, of which waited for: 8 -> 24; matrix products, arithmetic and copies ran while one was open for 4% -> 9% of each run, Pallas kernels for 0% -> 28%
where the time goes in v1:
time: 344 us; the launch traced here: 339 us
  Pallas kernels  112 us (33%)
  waiting for transfers between devices  107 us (31%)
  starting transfers between devices  50.9 us (15%)
  local copies, waits for them, and re-layouts  41.9 us (12%)
  other arithmetic  25.4 us (7%)
    pallas_call x20, Pallas kernels, call(): pl.pallas_call(body, out_shape=tuple(out_shape), in_specs=[SM] * smem + [...  112 us
    ppermute x66, waiting for transfers between devices, swap(): return lax.ppermute(a, axis, [(i, i ^ distance) for i in range(size)])  107 us
    ppermute x66, starting transfers between devices, swap(): return lax.ppermute(a, axis, [(i, i ^ distance) for i in range(size)])  49.3 us
    unnamed x198, local copies, waits for them, and re-layouts  35.3 us
    convert_element_type x23, other arithmetic, add_low(): return total.astype(BF)  11.3 us
    select_n x14, other arithmetic, in_order(): jnp.where(side == 0, jnp.concatenate([mine, got]), jnp.concatenate([got,...  10.5 us
  transfers between devices with their start and end apart: 68, of which 24 were waited for; matrix products, arithmetic and copies ran while one was open for 9% of the time, Pallas kernels for 28%

profile of v1, /device:TPU:0, one launch (start us, length us, event | category | flops | bytes accessed | tf_op | source)
XLA Modules:
  0.0 339.3 jit_solution(5321551739401304512)
XLA Ops:
  1.7 3.0 collective-permute-start.15
  18.5 5.6 %collective-permute-done.16 = bf16[96,768]{1,0:T(8,128)(2,1)S(1)} collective-permute-done((bf16[96,768]{1,0:T(8,128)(2,1)}, bf16[96,768]{1,0:T(8,128)(2,1)S(1)}, u32[]{:S(2)}, u32[]{:S(2)}) %collective-permute-start.16) | collective-permute-done | bytes 147488 | tf_op jit(solution)/shard_map/ppermute | solution.py:496
  26.1 14.0 %collective-permute-done.9 = bf16[48,768]{1,0:T(8,128)(2,1)} collective-permute-done((bf16[48,768]{1,0:T(8,128)(2,1)S(1)}, bf16[48,768]{1,0:T(8,128)(2,1)}, u32[]{:S(2)}, u32[]{:S(2)}) %collective-permute-start.9) | collective-permute-done | bytes 73760 | tf_op jit(solution)/shard_map/ppermute | solution.py:496
  44.3 5.3 %attend.4 = (bf16[512,192]{1,0:T(8,128)(2,1)S(1)}, f32[3,512]{1,0:T(4,128)S(1)}, bf16[512,192]{1,0:T(8,128)(2,1)S(1)}, bf16[1024,192]{1,0:T(8,128)(2,1)S(1)}, bf16[1024,192]{1,0:T(8,128)(2,1)S(1)}) custom-call(s32[4]{0:T(128)S(1)} %copy-done.83, s32[1]{0:T(128)} %bitcast.refs_1_.refs_0_, bf16[512,768]{1,0:T(8,128)(2,1)S(1)} %copy-done, ...), custom_call_target="tpu_custom_call" | custom-call | flops 1000 | bytes 1000 | tf_op jit(solution)/shard_map/attend/pallas_call | solution.py:52
  54.4 6.0 %attend.5 = (bf16[512,192]{1,0:T(8,128)(2,1)S(1)}, f32[3,512]{1,0:T(4,128)S(1)}, bf16[512,192]{1,0:T(8,128)(2,1)S(1)}, bf16[1024,192]{1,0:T(8,128)(2,1)S(1)}, bf16[1024,192]{1,0:T(8,128)(2,1)S(1)}) custom-call(s32[4]{0:T(128)S(1)} %copy-done.83, s32[1]{0:T(128)} %bitcast.refs_1_.refs_0_, bf16[512,768]{1,0:T(8,128)(2,1)S(1)} %copy-done, ...), custom_call_target="tpu_custom_call" | custom-call | flops 1000 | bytes 1000 | tf_op jit(solution)/shard_map/attend/pallas_call | solution.py:52
  65.0 5.7 %collective-permute-done.11 = bf16[96,768]{1,0:T(8,128)(2,1)S(1)} collective-permute-done((bf16[96,768]{1,0:T(8,128)(2,1)S(1)}, bf16[96,768]{1,0:T(8,128)(2,1)S(1)}, u32[]{:S(2)}, u32[]{:S(2)}) %collective-permute-start.11) | collective-permute-done | bytes 147488 | tf_op jit(solution)/shard_map/ppermute | solution.py:496
  72.0 18.0 %attend.6 = (bf16[512,192]{1,0:T(8,128)(2,1)S(1)}, f32[3,512]{1,0:T(4,128)S(1)}, bf16[512,192]{1,0:T(8,128)(2,1)S(1)}, bf16[1024,192]{1,0:T(8,128)(2,1)S(1)}, bf16[1024,192]{1,0:T(8,128)(2,1)S(1)}) custom-call(s32[4]{0:T(128)S(1)} %copy-done.83, s32[1]{0:T(128)} %bitcast.refs_1_.refs_0_, bf16[512,768]{1,0:T(8,128)(2,1)S(1)} %copy-done, ...), custom_call_target="tpu_custom_call" | custom-call | flops 1000 | bytes 1000 | tf_op jit(solution)/shard_map/attend/pallas_call | solution.py:52
  95.2 5.3 %attend.7 = (bf16[512,192]{1,0:T(8,128)(2,1)S(1)}, f32[3,512]{1,0:T(4,128)S(1)}, bf16[512,192]{1,0:T(8,128)(2,1)S(1)}, bf16[1024,192]{1,0:T(8,128)(2,1)S(1)}, bf16[1024,192]{1,0:T(8,128)(2,1)S(1)}) custom-call(s32[4]{0:T(128)S(1)} %copy-done.83, s32[1]{0:T(128)} %bitcast.refs_1_.refs_0_, bf16[512,768]{1,0:T(8,128)(2,1)S(1)} %copy-done, ...), custom_call_target="tpu_custom_call" | custom-call | flops 1000 | bytes 1000 | tf_op jit(solution)/shard_map/attend/pallas_call | solution.py:52
  108.7 5.6 %ffn_near.1 = (bf16[512,768]{1,0:T(8,128)(2,1)S(1)}, bf16[512,768]{1,0:T(8,128)(2,1)S(1)}, bf16[512,768]{1,0:T(8,128)(2,1)S(1)}, bf16[512,768]{1,0:T(8,128)(2,1)S(1)}, f32[512,768]{1,0:T(8,128)S(1)}) custom-call(bf16[512,768]{1,0:T(8,128)(2,1)S(1)} %get-tuple-element.135.refs_0_.refs_1_, bf16[592,768]{1,0:T(8,128)(2,1)S(1)} %copy-done.6, ...), custom_call_target="tpu_custom_call" | custom-call | flops 1000 | bytes 1000 | tf_op jit(solution)/shard_map/ffn_near/pallas_call | solution.py:52
  119.2 9.0 %ffn_far.1 = (bf16[512,768]{1,0:T(8,128)(2,1)S(1)}, bf16[512,768]{1,0:T(8,128)(2,1)S(1)}, bf16[512,768]{1,0:T(8,128)(2,1)S(1)}, bf16[512,768]{1,0:T(8,128)(2,1)S...) custom-call(bf16[512,768]{1,0:T(8,128)(2,1)S(1)} %get-tuple-element., ...), custom_call_target="tpu_custom_call" | custom-call | flops 1000 | bytes 1000 | tf_op jit(solution)/shard_map/ffn_far/pallas_call | solution.py:52
  128.1 4.1 %ffn_back.4 = (bf16[768,768]{1,0:T(8,128)(2,1)}, bf16[768,768]{1,0:T(8,128)(2,1)}, f32[1,768]{1,0:T(1,128)S(1)}, f32[512,768]{1,0:T(8,128)S(1)}) custom-call(bf16[512,768]{1,0:T(8,128)(2,1)S(1)} %get-tuple-element.150.refs_0_, bf16[512,768]{1,0:T(8,128)(2,1)S(1)} %get-tuple-element.135.refs_0_.refs_1_, ...), custom_call_target="tpu_custom_call", output_to_operand_aliasing={{3}: (4, {})} | custom-call | flops 1000 | bytes 1000 | tf_op jit(solution)/shard_map/ffn_back/pallas_call | solution.py:52
  141.1 4.1 %ffn_back.5 = (bf16[768,768]{1,0:T(8,128)(2,1)S(1)}, bf16[768,768]{1,0:T(8,128)(2,1)S(1)}, f32[1,768]{1,0:T(1,128)S(1)}, f32[512,768]{1,0:T(8,128)S(1)}) custom-call(bf16[512,768]{1,0:T(8,128)(2,1)S(1)} %copy-done.9, bf16[512,768]{1,0:T(8,128)(2,1)S(1)} %get-tuple-element.135.refs_0_.refs_1_, ...), custom_call_target="tpu_custom_call", output_to_operand_aliasing={{3}: (4, {})} | custom-call | flops 1000 | bytes 1000 | tf_op jit(solution)/shard_map/ffn_back/pallas_call | solution.py:52
  145.3 3.4 %ffn_back.6 = (bf16[768,768]{1,0:T(8,128)(2,1)}, bf16[768,768]{1,0:T(8,128)(2,1)}, f32[1,768]{1,0:T(1,128)S(1)}, f32[512,768]{1,0:T(8,128)S(1)}) custom-call(bf16[512,768]{1,0:T(8,128)(2,1)S(1)} %copy-done.9, bf16[512,768]{1,0:T(8,128)(2,1)S(1)} %get-tuple-element.135.refs_0_.refs_1_, ...), custom_call_target="tpu_custom_call", output_to_operand_aliasing={{3}: (4, {})} | custom-call | flops 1000 | bytes 1000 | tf_op jit(solution)/shard_map/ffn_back/pallas_call | solution.py:52
  165.5 2.9 ffn_back.7
  175.4 9.8 %attend_back.4 = (bf16[384,768]{1,0:T(8,128)(2,1)S(1)}, bf16[384,768]{1,0:T(8,128)(2,1)S(1)}, f32[512,768]{1,0:T(8,128)S(1)}, f32[512,768]{1,0:T(8,128)S(1)}, f3...) custom-call(s32[4]{0:T(128)S(1)} %copy-done.83, ...), custom_call_target="tpu_custom_call", output_to_operand_aliasing={{2}: (13, {}), {3}: (14, {})} | custom-call | flops 1000 | bytes 1000 | tf_op jit(solution)/shard_map/attend_back/pallas_call | solution.py:52
  185.8 10.7 %attend_back.5 = (bf16[384,768]{1,0:T(8,128)(2,1)S(1)}, bf16[384,768]{1,0:T(8,128)(2,1)S(1)}, f32[512,768]{1,0:T(8,128)S(1)}, f32[512,768]{1,0:T(8,128)S(1)}, f3...) custom-call(s32[4]{0:T(128)S(1)} %copy-done.83, ...), custom_call_target="tpu_custom_call", output_to_operand_aliasing={{2}: (13, {}), {3}: (14, {})} | custom-call | flops 1000 | bytes 1000 | tf_op jit(solution)/shard_map/attend_back/pallas_call | solution.py:52
  196.6 3.5 %collective-permute-start.33 = (bf16[96,768]{1,0:T(8,128)(2,1)S(1)}, bf16[96,768]{1,0:T(8,128)(2,1)S(1)}, u32[]{:S(2)}, u32[]{:S(2)}) collective-permute-start(bf16[96,768]{1,0:T(8,128)(2,1)S(1)} %constant_dynamic-slice_fusion.10), channel_id=1, source_target_pairs={{0,16},{4,20},{8,24},{12,28},{16,0},{20,4},{24,8},{28,12},{1,17},{... | collective-permute-start | bytes 442376 | tf_op jit(solution)/shard_map/ppermute | solution.py:496
  203.2 4.2 %collective-permute-done.33.refs_16_ = bf16[96,768]{1,0:T(8,128)(2,1)S(1)} collective-permute-done((bf16[96,768]{1,0:T(8,128)(2,1)S(1)}, bf16[96,768]{1,0:T(8,128)(2,1)S(1)}, u32[]{:S(2)}, u32[]{:S(2)}) %collective-permute-start.33) | collective-permute-done | bytes 147488 | tf_op jit(solution)/shard_map/ppermute | solution.py:496
  210.2 10.8 %attend_back.6 = (bf16[384,768]{1,0:T(8,128)(2,1)S(1)}, bf16[384,768]{1,0:T(8,128)(2,1)S(1)}, f32[512,768]{1,0:T(8,128)S(1)}, f32[512,768]{1,0:T(8,128)S(1)}, f3...) custom-call(s32[4]{0:T(128)S(1)} %copy-done.83, ...), custom_call_target="tpu_custom_call", output_to_operand_aliasing={{2}: (13, {}), {3}: (14, {})} | custom-call | flops 1000 | bytes 1000 | tf_op jit(solution)/shard_map/attend_back/pallas_call | solution.py:52
  223.6 10.4 %attend_back.7 = (bf16[384,768]{1,0:T(8,128)(2,1)S(1)}, bf16[384,768]{1,0:T(8,128)(2,1)S(1)}, f32[512,768]{1,0:T(8,128)S(1)}, f32[512,768]{1,0:T(8,128)S(1)}, f3...) custom-call(s32[4]{0:T(128)S(1)} %copy-done.83, ...), custom_call_target="tpu_custom_call", output_to_operand_aliasing={{2}: (13, {}), {3}: (14, {})} | custom-call | flops 1000 | bytes 1000 | tf_op jit(solution)/shard_map/attend_back/pallas_call | solution.py:52
  237.2 4.2 %collective-permute-done.45 = f32[24,768]{1,0:T(8,128)S(1)} collective-permute-done((f32[24,768]{1,0:T(8,128)S(1)}, f32[24,768]{1,0:T(8,128)S(1)}, u32[]{:S(2)}, u32[]{:S(2)}) %collective-permute-start.45) | collective-permute-done | bytes 73760 | tf_op jit(solution)/shard_map/ppermute | solution.py:496
  241.7 2.9 collective-permute-done.63
  244.7 9.0 %collective-permute-done.59 = bf16[96,768]{1,0:T(8,128)(2,1)S(1)} collective-permute-done((bf16[96,768]{1,0:T(8,128)(2,1)S(1)}, bf16[96,768]{1,0:T(8,128)(2,1)S(1)}, u32[]{:S(2)}, u32[]{:S(2)}) %collective-permute-start.59) | collective-permute-done | bytes 147488 | tf_op jit(solution)/shard_map/ppermute | solution.py:496
  254.5 3.5 %collective-permute-done.46 = f32[24,768]{1,0:T(8,128)S(1)} collective-permute-done((f32[24,768]{1,0:T(8,128)S(1)}, f32[24,768]{1,0:T(8,128)S(1)}, u32[]{:S(2)}, u32[]{:S(2)}) %collective-permute-start.46) | collective-permute-done | bytes 73760 | tf_op jit(solution)/shard_map/ppermute | solution.py:496
  262.5 4.4 %collective-permute-done.47 = f32[24,768]{1,0:T(8,128)S(1)} collective-permute-done((f32[24,768]{1,0:T(8,128)S(1)}, f32[24,768]{1,0:T(8,128)S(1)}, u32[]{:S(2)}, u32[]{:S(2)}) %collective-permute-start.47) | collective-permute-done | bytes 73760 | tf_op jit(solution)/shard_map/ppermute | solution.py:496
  270.5 3.1 collective-permute-done.65
  274.6 7.9 %collective-permute-done.51 = bf16[192,768]{1,0:T(8,128)(2,1)S(1)} collective-permute-done((bf16[192,768]{1,0:T(8,128)(2,1)S(1)}, bf16[192,768]{1,0:T(8,128)(2,1)S(1)}, u32[]{:S(2)}, u32[]{:S(2)}) %collective-permute-start.51) | collective-permute-done | bytes 294944 | tf_op jit(solution)/shard_map/ppermute | solution.py:496
  285.0 7.5 %collective-permute-done.66 = bf16[192,768]{1,0:T(8,128)(2,1)S(1)} collective-permute-done((bf16[192,768]{1,0:T(8,128)(2,1)S(1)}, bf16[192,768]{1,0:T(8,128)(2,1)S(1)}, u32[]{:S(2)}, u32[]{:S(2)}) %collective-permute-start.66) | collective-permute-done | bytes 294944 | tf_op jit(solution)/shard_map/ppermute | solution.py:496
  298.8 6.2 %collective-permute-done.40 = bf16[48,768]{1,0:T(8,128)(2,1)S(1)} collective-permute-done((bf16[48,768]{1,0:T(8,128)(2,1)S(1)}, bf16[48,768]{1,0:T(8,128)(2,1)S(1)}, u32[]{:S(2)}, u32[]{:S(2)}) %collective-permute-start.40) | collective-permute-done | bytes 73760 | tf_op jit(solution)/shard_map/ppermute | solution.py:496
  305.1 6.2 %collective-permute-done.53 = bf16[48,768]{1,0:T(8,128)(2,1)S(1)} collective-permute-done((bf16[48,768]{1,0:T(8,128)(2,1)S(1)}, bf16[48,768]{1,0:T(8,128)(2,1)S(1)}, u32[]{:S(2)}, u32[]{:S(2)}) %collective-permute-start.53) | collective-permute-done | bytes 73760 | tf_op jit(solution)/shard_map/ppermute | solution.py:496
  312.1 4.9 %collective-permute-done.41 = bf16[48,768]{1,0:T(8,128)(2,1)S(1)} collective-permute-done((bf16[48,768]{1,0:T(8,128)(2,1)S(1)}, bf16[48,768]{1,0:T(8,128)(2,1)S(1)}, u32[]{:S(2)}, u32[]{:S(2)}) %collective-permute-start.41) | collective-permute-done | bytes 73760 | tf_op jit(solution)/shard_map/ppermute | solution.py:496
  317.0 5.8 %collective-permute-done.54 = bf16[48,768]{1,0:T(8,128)(2,1)S(1)} collective-permute-done((bf16[48,768]{1,0:T(8,128)(2,1)S(1)}, bf16[48,768]{1,0:T(8,128)(2,1)S(1)}, u32[]{:S(2)}, u32[]{:S(2)}) %collective-permute-start.54) | collective-permute-done | bytes 73760 | tf_op jit(solution)/shard_map/ppermute | solution.py:496
  (390 shorter events, 129.7 us)
Async XLA Ops:
  4.7 37.0 %collective-permute-start = (bf16[512,768]{1,0:T(8,128)(2,1)}, bf16[512,768]{1,0:T(8,128)(2,1)S(1)}, u32[]{:S(2)}, u32[]{:S(2)}) collective-permute-start(bf16[512,768]{1,0:T(8,128)(2,1)} %refs_2_.15), channel_id=1, source_target_pairs={{0,1},{1,0},{2,3},{3,2},{4,5},{5,4},{6,7},{7,6},{8,9},{9,8},{10,11... | collective-permute-start | bytes 2359304 | tf_op jit(solution)/shard_map/ppermute | solution.py:496
  4.7 39.5 %collective-permute-start.1 = (bf16[512,768]{1,0:T(8,128)(2,1)}, bf16[512,768]{1,0:T(8,128)(2,1)S(1)}, u32[]{:S(2)}, u32[]{:S(2)}) collective-permute-start(bf16[512,768]{1,0:T(8,128)(2,1)} %refs_2_.15), channel_id=1, source_target_pairs={{1,2},{2,1},{5,6},{6,5},{9,10},{10,9},{13,14},{14,13},{17,18},{18,... | collective-permute-start | bytes 2359304 | tf_op jit(solution)/shard_map/ppermute | solution.py:508
  10.4 44.0 %collective-permute-start.2 = (bf16[592,768]{1,0:T(8,128)(2,1)S(1)}, bf16[592,768]{1,0:T(8,128)(2,1)}, u32[]{:S(2)}, u32[]{:S(2)}) collective-permute-start(bf16[592,768]{1,0:T(8,128)(2,1)S(1)} %pack_joint.1.refs_5_.refs_1_), channel_id=1, source_target_pairs={{0,1},{1,0},{2,3},{3,2},{4,5},{5,4},{6,7},{7,6},{8,9},{9,8},{10,11... | collective-permute-start | bytes 2727944 | tf_op jit(solution)/shard_map/ppermute | solution.py:496
  12.2 51.2 %collective-permute-start.3 = (bf16[592,768]{1,0:T(8,128)(2,1)S(1)}, bf16[592,768]{1,0:T(8,128)(2,1)}, u32[]{:S(2)}, u32[]{:S(2)}) collective-permute-start(bf16[592,768]{1,0:T(8,128)(2,1)S(1)} %pack_joint.1.refs_5_.refs_1_), channel_id=1, source_target_pairs={{0,2},{1,3},{2,0},{3,1},{4,6},{5,7},{6,4},{7,5},{8,10},{9,11},{10,... | collective-permute-start | bytes 2727944 | tf_op jit(solution)/shard_map/ppermute | solution.py:496
  24.1 16.0 %collective-permute-start.9 = (bf16[48,768]{1,0:T(8,128)(2,1)S(1)}, bf16[48,768]{1,0:T(8,128)(2,1)}, u32[]{:S(2)}, u32[]{:S(2)}) collective-permute-start(bf16[48,768]{1,0:T(8,128)(2,1)S(1)} %constant_dynamic-slice_fusion.16), channel_id=1, source_target_pairs={{0,2},{1,3},{2,0},{3,1},{4,6},{5,7},{6,4},{7,5},{8,10},{9,11},{10,... | collective-permute-start | bytes 221192 | tf_op jit(solution)/shard_map/ppermute | solution.py:496
  41.7 21.8 %collective-permute-start.10 = (bf16[48,768]{1,0:T(8,128)(2,1)}, bf16[48,768]{1,0:T(8,128)(2,1)S(1)}, u32[]{:S(2)}, u32[]{:S(2)}) collective-permute-start(bf16[48,768]{1,0:T(8,128)(2,1)} %collective-permute-done.9), channel_id=1, source_target_pairs={{0,16},{4,20},{8,24},{12,28},{16,0},{20,4},{24,8},{28,12},{1,17},{... | collective-permute-start | bytes 221192 | tf_op jit(solution)/shard_map/ppermute | solution.py:496
  52.9 37.2 %collective-permute-start.18 = (bf16[384,768]{1,0:T(8,128)(2,1)}, bf16[384,768]{1,0:T(8,128)(2,1)}, u32[]{:S(2)}, u32[]{:S(2)}) collective-permute-start(bf16[384,768]{1,0:T(8,128)(2,1)} %maximum_select_fusion.4), channel_id=1, source_target_pairs={{0,4},{4,0},{8,12},{12,8},{16,20},{20,16},{24,28},{28,24},{1,5},{5... | collective-permute-start | bytes 1769480 | tf_op jit(solution)/shard_map/ppermute | solution.py:496
  63.4 30.0 %collective-permute-start.4 = (bf16[592,768]{1,0:T(8,128)(2,1)}, bf16[592,768]{1,0:T(8,128)(2,1)S(1)}, u32[]{:S(2)}, u32[]{:S(2)}) collective-permute-start(bf16[592,768]{1,0:T(8,128)(2,1)} %collective-permute-done.3.refs_5_.refs_1_), channel_id=1, source_target_pairs={{0,1},{1,0},{2,3},{3,2},{4,5},{5,4},{6,7},{7,6},{8,9},{9,8},{10,11... | collective-permute-start | bytes 2727944 | tf_op jit(solution)/shard_map/ppermute | solution.py:496
  65.0 27.7 %collective-permute-start.6 = (bf16[192,768]{1,0:T(8,128)(2,1)}, bf16[192,768]{1,0:T(8,128)(2,1)}, u32[]{:S(2)}, u32[]{:S(2)}) collective-permute-start(bf16[192,768]{1,0:T(8,128)(2,1)} %refs_6_.3), channel_id=1, source_target_pairs={{0,2},{1,3},{2,0},{3,1},{4,6},{5,7},{6,4},{7,5},{8,10},{9,11},{10,... | collective-permute-start | bytes 884744 | tf_op jit(solution)/shard_map/ppermute | solution.py:496
  70.8 22.5 %collective-permute-start.8 = (bf16[384,768]{1,0:T(8,128)(2,1)}, bf16[384,768]{1,0:T(8,128)(2,1)}, u32[]{:S(2)}, u32[]{:S(2)}) collective-permute-start(bf16[384,768]{1,0:T(8,128)(2,1)} %get-tuple-element.136), channel_id=1, source_target_pairs={{0,2},{1,3},{2,0},{3,1},{4,6},{5,7},{6,4},{7,5},{8,10},{9,11},{10,... | collective-permute-start | bytes 1769480 | tf_op jit(solution)/shard_map/ppermute | solution.py:496
  71.5 21.3 %collective-permute-start.12 = (bf16[192,768]{1,0:T(8,128)(2,1)}, bf16[192,768]{1,0:T(8,128)(2,1)}, u32[]{:S(2)}, u32[]{:S(2)}) collective-permute-start(bf16[192,768]{1,0:T(8,128)(2,1)} %maximum_select_fusion.9), channel_id=1, source_target_pairs={{0,4},{4,0},{8,12},{12,8},{16,20},{20,16},{24,28},{28,24},{1,5},{5... | collective-permute-start | bytes 884744 | tf_op jit(solution)/shard_map/ppermute | solution.py:496
  90.1 18.5 %collective-permute-start.20 = (bf16[768,768]{1,0:T(8,128)(2,1)S(1)}, bf16[768,768]{1,0:T(8,128)(2,1)S(1)}, u32[]{:S(2)}, u32[]{:S(2)}) collective-permute-start(bf16[768,768]{1,0:T(8,128)(2,1)S(1)} %copy-done.12), channel_id=1, source_target_pairs={{0,1},{1,0},{2,3},{3,2},{4,5},{5,4},{6,7},{7,6},{8,9},{9,8},{10,11... | collective-permute-start | bytes 3538952 | tf_op jit(solution)/shard_map/ppermute | solution.py:496
  92.8 26.3 %collective-permute-start.19 = (bf16[768,768]{1,0:T(8,128)(2,1)S(1)}, bf16[768,768]{1,0:T(8,128)(2,1)S(1)}, u32[]{:S(2)}, u32[]{:S(2)}) collective-permute-start(bf16[768,768]{1,0:T(8,128)(2,1)S(1)} %maximum_select_fusion.refs_7_.refs_5_), channel_id=1, source_target_pairs={{0,1},{1,0},{2,3},{3,2},{4,5},{5,4},{6,7},{7,6},{8,9},{9,8},{10,11... | collective-permute-start | bytes 3538952 | tf_op jit(solution)/shard_map/ppermute | solution.py:496
  148.7 21.5 %collective-permute-start.24 = (bf16[768,768]{1,0:T(8,128)(2,1)}, bf16[768,768]{1,0:T(8,128)(2,1)}, u32[]{:S(2)}, u32[]{:S(2)}) collective-permute-start(bf16[768,768]{1,0:T(8,128)(2,1)} %get-tuple-element.167), channel_id=1, source_target_pairs={{0,1},{1,0},{2,3},{3,2},{4,5},{5,4},{6,7},{7,6},{8,9},{9,8},{10,11... | collective-permute-start | bytes 3538952 | tf_op jit(solution)/shard_map/ppermute | solution.py:496
  151.8 16.6 %collective-permute-start.26 = (bf16[384,768]{1,0:T(8,128)(2,1)}, bf16[384,768]{1,0:T(8,128)(2,1)}, u32[]{:S(2)}, u32[]{:S(2)}) collective-permute-start(bf16[384,768]{1,0:T(8,128)(2,1)} %constant_dynamic-slice_fusion.14), channel_id=1, source_target_pairs={{0,4},{4,0},{8,12},{12,8},{16,20},{20,16},{24,28},{28,24},{1,5},{5... | collective-permute-start | bytes 1769480 | tf_op jit(solution)/shard_map/ppermute | solution.py:496
  153.4 20.7 %collective-permute-start.25 = (bf16[768,768]{1,0:T(8,128)(2,1)}, bf16[768,768]{1,0:T(8,128)(2,1)}, u32[]{:S(2)}, u32[]{:S(2)}) collective-permute-start(bf16[768,768]{1,0:T(8,128)(2,1)} %get-tuple-element.182), channel_id=1, source_target_pairs={{0,1},{1,0},{2,3},{3,2},{4,5},{5,4},{6,7},{7,6},{8,9},{9,8},{10,11... | collective-permute-start | bytes 3538952 | tf_op jit(solution)/shard_map/ppermute | solution.py:496
  156.1 44.1 %collective-permute-start.29 = (bf16[768,768]{1,0:T(8,128)(2,1)}, bf16[768,768]{1,0:T(8,128)(2,1)}, u32[]{:S(2)}, u32[]{:S(2)}) collective-permute-start(bf16[768,768]{1,0:T(8,128)(2,1)} %add_convert_fusion.1), channel_id=1, source_target_pairs={{0,2},{1,3},{2,0},{3,1},{4,6},{5,7},{6,4},{7,5},{8,10},{9,11},{10,... | collective-permute-start | bytes 3538952 | tf_op jit(solution)/shard_map/ppermute | solution.py:496
  169.7 26.8 %collective-permute-start.28 = (bf16[192,768]{1,0:T(8,128)(2,1)S(1)}, bf16[192,768]{1,0:T(8,128)(2,1)S(1)}, u32[]{:S(2)}, u32[]{:S(2)}) collective-permute-start(bf16[192,768]{1,0:T(8,128)(2,1)S(1)} %constant_dynamic-slice_fusion.12), channel_id=1, source_target_pairs={{0,8},{4,12},{8,0},{12,4},{16,24},{20,28},{24,16},{28,20},{1,9},{5... | collective-permute-start | bytes 884744 | tf_op jit(solution)/shard_map/ppermute | solution.py:496
  172.0 36.7 %collective-permute-start.27 = (bf16[384,768]{1,0:T(8,128)(2,1)S(1)}, bf16[384,768]{1,0:T(8,128)(2,1)S(1)}, u32[]{:S(2)}, u32[]{:S(2)}) collective-permute-start(bf16[384,768]{1,0:T(8,128)(2,1)S(1)} %constant_dynamic-slice_fusion.13), channel_id=1, source_target_pairs={{0,4},{4,0},{8,12},{12,8},{16,20},{20,16},{24,28},{28,24},{1,5},{5... | collective-permute-start | bytes 1769480 | tf_op jit(solution)/shard_map/ppermute | solution.py:496
  185.2 23.8 %collective-permute-start.30 = (bf16[384,768]{1,0:T(8,128)(2,1)S(1)}, bf16[384,768]{1,0:T(8,128)(2,1)S(1)}, u32[]{:S(2)}, u32[]{:S(2)}) collective-permute-start(bf16[384,768]{1,0:T(8,128)(2,1)S(1)} %get-tuple-element.190), channel_id=1, source_target_pairs={{0,1},{1,0},{2,3},{3,2},{4,5},{5,4},{6,7},{7,6},{8,9},{9,8},{10,11... | collective-permute-start | bytes 1769480 | tf_op jit(solution)/shard_map/ppermute | solution.py:496
  185.3 24.9 %collective-permute-start.31 = (bf16[384,768]{1,0:T(8,128)(2,1)S(1)}, bf16[384,768]{1,0:T(8,128)(2,1)S(1)}, u32[]{:S(2)}, u32[]{:S(2)}) collective-permute-start(bf16[384,768]{1,0:T(8,128)(2,1)S(1)} %get-tuple-element.191), channel_id=1, source_target_pairs={{0,1},{1,0},{2,3},{3,2},{4,5},{5,4},{6,7},{7,6},{8,9},{9,8},{10,11... | collective-permute-start | bytes 1769480 | tf_op jit(solution)/shard_map/ppermute | solution.py:496
  202.3 18.8 %collective-permute-start.57 = (bf16[384,768]{1,0:T(8,128)(2,1)S(1)}, bf16[384,768]{1,0:T(8,128)(2,1)S(1)}, u32[]{:S(2)}, u32[]{:S(2)}) collective-permute-start(bf16[384,768]{1,0:T(8,128)(2,1)S(1)} %constant_dynamic-slice_fusion.3), channel_id=1, source_target_pairs={{0,4},{4,0},{8,12},{12,8},{16,20},{20,16},{24,28},{28,24},{1,5},{5... | collective-permute-start | bytes 1769480 | tf_op jit(solution)/shard_map/ppermute | solution.py:496
  207.5 34.1 %collective-permute-start.64 = (bf16[96,768]{1,0:T(8,128)(2,1)S(1)}, bf16[96,768]{1,0:T(8,128)(2,1)S(1)}, u32[]{:S(2)}, u32[]{:S(2)}) collective-permute-start(bf16[96,768]{1,0:T(8,128)(2,1)S(1)} %add_convert_fusion.17), channel_id=1, source_target_pairs={{0,2},{1,3},{2,0},{3,1},{4,6},{5,7},{6,4},{7,5},{8,10},{9,11},{10,... | collective-permute-start | bytes 442376 | tf_op jit(solution)/shard_map/ppermute | solution.py:496
  209.1 48.9 %collective-permute-start.37 = (bf16[384,768]{1,0:T(8,128)(2,1)S(1)}, bf16[384,768]{1,0:T(8,128)(2,1)S(1)}, u32[]{:S(2)}, u32[]{:S(2)}) collective-permute-start(bf16[384,768]{1,0:T(8,128)(2,1)S(1)} %add_convert_fusion.8), channel_id=1, source_target_pairs={{0,2},{1,3},{2,0},{3,1},{4,6},{5,7},{6,4},{7,5},{8,10},{9,11},{10,... | collective-permute-start | bytes 1769480 | tf_op jit(solution)/shard_map/ppermute | solution.py:496
  221.1 37.1 %collective-permute-start.36 = (bf16[384,768]{1,0:T(8,128)(2,1)S(1)}, bf16[384,768]{1,0:T(8,128)(2,1)S(1)}, u32[]{:S(2)}, u32[]{:S(2)}) collective-permute-start(bf16[384,768]{1,0:T(8,128)(2,1)S(1)} %get-tuple-element.200), channel_id=1, source_target_pairs={{0,1},{1,0},{2,3},{3,2},{4,5},{5,4},{6,7},{7,6},{8,9},{9,8},{10,11... | collective-permute-start | bytes 1769480 | tf_op jit(solution)/shard_map/ppermute | solution.py:496
  241.5 19.8 %collective-permute-start.50 = (bf16[384,768]{1,0:T(8,128)(2,1)S(1)}, bf16[384,768]{1,0:T(8,128)(2,1)S(1)}, u32[]{:S(2)}, u32[]{:S(2)}) collective-permute-start(bf16[384,768]{1,0:T(8,128)(2,1)S(1)} %add_convert_fusion.6), channel_id=1, source_target_pairs={{0,2},{1,3},{2,0},{3,1},{4,6},{5,7},{6,4},{7,5},{8,10},{9,11},{10,... | collective-permute-start | bytes 1769480 | tf_op jit(solution)/shard_map/ppermute | solution.py:496
  241.6 19.8 %collective-permute-start.49 = (bf16[384,768]{1,0:T(8,128)(2,1)S(1)}, bf16[384,768]{1,0:T(8,128)(2,1)S(1)}, u32[]{:S(2)}, u32[]{:S(2)}) collective-permute-start(bf16[384,768]{1,0:T(8,128)(2,1)S(1)} %get-tuple-element.221), channel_id=1, source_target_pairs={{0,1},{1,0},{2,3},{3,2},{4,5},{5,4},{6,7},{7,6},{8,9},{9,8},{10,11... | collective-permute-start | bytes 1769480 | tf_op jit(solution)/shard_map/ppermute | solution.py:496
  258.0 64.9 %collective-permute-start.34 = (bf16[512,768]{1,0:T(8,128)(2,1)S(1)}, bf16[512,768]{1,0:T(8,128)(2,1)S(1)}, u32[]{:S(2)}, u32[]{:S(2)}) collective-permute-start(bf16[512,768]{1,0:T(8,128)(2,1)S(1)} %convert_element_type.258), channel_id=1, source_target_pairs={{0,1},{1,0},{2,3},{3,2},{4,5},{5,4},{6,7},{7,6},{8,9},{9,8},{10,11... | collective-permute-start | bytes 2359304 | tf_op jit(solution)/shard_map/ppermute | solution.py:496
  266.9 58.6 %collective-permute-start.35 = (bf16[512,768]{1,0:T(8,128)(2,1)S(1)}, bf16[512,768]{1,0:T(8,128)(2,1)S(1)}, u32[]{:S(2)}, u32[]{:S(2)}) collective-permute-start(bf16[512,768]{1,0:T(8,128)(2,1)S(1)} %convert_element_type.258), channel_id=1, source_target_pairs={{1,2},{2,1},{5,6},{6,5},{9,10},{10,9},{13,14},{14,13},{17,18},{18,... | collective-permute-start | bytes 2359304 | tf_op jit(solution)/shard_map/ppermute | solution.py:508
  270.4 40.9 %collective-permute-start.48 = (f32[24,768]{1,0:T(8,128)S(1)}, f32[24,768]{1,0:T(8,128)S(1)}, u32[]{:S(2)}, u32[]{:S(2)}) collective-permute-start(f32[24,768]{1,0:T(8,128)S(1)} %add.194), channel_id=1, source_target_pairs={{0,16},{4,20},{8,24},{12,28},{16,0},{20,4},{24,8},{28,12},{1,17},{... | collective-permute-start | bytes 221192 | tf_op jit(solution)/shard_map/ppermute | solution.py:496
  295.4 34.9 %collective-permute-start.62 = (bf16[384,768]{1,0:T(8,128)(2,1)S(1)}, bf16[384,768]{1,0:T(8,128)(2,1)S(1)}, u32[]{:S(2)}, u32[]{:S(2)}) collective-permute-start(bf16[384,768]{1,0:T(8,128)(2,1)S(1)} %maximum_select_fusion.7), channel_id=1, source_target_pairs={{0,4},{4,0},{8,12},{12,8},{16,20},{20,16},{24,28},{28,24},{1,5},{5... | collective-permute-start | bytes 1769480 | tf_op jit(solution)/shard_map/ppermute | solution.py:496
  311.4 20.6 %collective-permute-start.67 = (bf16[384,768]{1,0:T(8,128)(2,1)S(1)}, bf16[384,768]{1,0:T(8,128)(2,1)S(1)}, u32[]{:S(2)}, u32[]{:S(2)}) collective-permute-start(bf16[384,768]{1,0:T(8,128)(2,1)S(1)} %maximum_select_fusion.8), channel_id=1, source_target_pairs={{0,4},{4,0},{8,12},{12,8},{16,20},{20,16},{24,28},{28,24},{1,5},{5... | collective-permute-start | bytes 1769480 | tf_op jit(solution)/shard_map/ppermute | solution.py:496
  (135 other events, 839.9 us)
